TPU v7x, 32 devices: a whole 2x2x4 slice. The times are simulated.
32 devices in a mesh: rows: 8 (over y, x, core), chan: 4 (over z).
Axes of the slice: x: 2, y: 2, z: 4, core: 2. Of those that a mesh axis runs over, the one named last changes fastest.
Arguments:
- features: bfloat16 [1024, 1, 4096], P('chan', None, 'rows'), may hold values from -24 to 24
- gain_first: float32 [1024], P('chan'), may hold values from 0.1 to 1.9
- weight_first: bfloat16 [3, 3, 3, 1024, 1024], P(None, None, None, 'chan'), may hold values from -0.0390625 to 0.0390625
- bias_first: float32 [1024], P('chan'), may hold values from -3 to 3
- gain_second: float32 [1024], P('chan'), may hold values from 0.1 to 1.9
- weight_second: bfloat16 [3, 3, 3, 1024, 1024], P(None, None, None, 'chan'), may hold values from -0.0390625 to 0.0390625
- bias_second: float32 [1024], P('chan'), may hold values from -3 to 3
Outputs:
- block_out: bfloat16 [1024, 1, 4096], P('chan', None, 'rows')
All inputs are finite; a program needn't handle non-finite values.
Results may differ from a plain program's by a relative error of at most 0.0022.
Values may be sent and summed in bfloat16 or wider, within the bound.
No kernel may reach another device: no remote copies, remote signals or barrier semaphores. Data moves between devices by JAX's collectives and lax.ppermute only.
A program may use at most 64 MiB of HBM per device.

v0:
```python
import jax
import jax.numpy as jnp
from jax import lax
from jax.sharding import PartitionSpec as P

CH = 1024
WIDTH = 64


def padded(block, sides, width):
    for axis, dim in sides:
        count = lax.axis_size(axis)
        forward = [(i, i + 1) for i in range(count - 1)]
        backward = [(target, source) for source, target in forward]
        low = lax.ppermute(
            lax.slice_in_dim(block, block.shape[dim] - width, None, axis=dim), axis, forward
        )
        high = lax.ppermute(lax.slice_in_dim(block, 0, width, axis=dim), axis, backward)
        block = jnp.concatenate([low, block, high], axis=dim)
    return block


def conv_rows(data, kernel):
    channels, frames, cells = data.shape
    rows_in = cells // WIDTH
    grid = data.reshape(1, channels, frames, rows_in, WIDTH)
    result = lax.conv_general_dilated(
        grid,
        kernel,
        (1, 1, 1),
        ((2, 0), (0, 0), (1, 1)),
        dimension_numbers=("NCDHW", "DHWOI", "NCDHW"),
        preferred_element_type=jnp.float32,
    )
    return result[0].astype(jnp.float32).reshape(kernel.shape[3], frames, (rows_in - 2) * WIDTH)


def activate(values, gain):
    totals = lax.psum(jnp.sum(values * values, axis=0), "chan")
    mean_sq = (totals / CH)[None]
    return jax.nn.silu(values * gain[:, None, None] / jnp.sqrt(mean_sq + 1e-06)).astype(
        jnp.bfloat16
    )


def convolve(block, width, kernel):
    whole = lax.all_gather(block, "chan", axis=0, tiled=True)
    whole = padded(whole, (("rows", 2),), width * WIDTH)
    return conv_rows(whole, kernel)


def on_device(
    features, gain_first, weight_first, bias_first, gain_second, weight_second, bias_second
):
    source = features.astype(jnp.float32)
    first = activate(source, gain_first)
    middle = convolve(first, 1, weight_first) + bias_first[:, None, None]
    second = activate(middle, gain_second)
    result = convolve(second, 1, weight_second)
    return (source + result + bias_second[:, None, None]).astype(jnp.bfloat16)


def solution(mesh):
    in_specs = (
        P("chan", None, "rows"),
        P("chan"),
        P(None, None, None, "chan", None),
        P("chan"),
        P("chan"),
        P(None, None, None, "chan", None),
        P("chan"),
    )
    out_specs = P("chan", None, "rows")
    return jax.shard_map(
        on_device, mesh=mesh, in_specs=in_specs, out_specs=out_specs, check_vma=False
    )
```

profile of v0, /device:TPU:3, one launch (start us, length us, event | category | flops | bytes accessed | tf_op | source)
XLA Modules:
  0.0 154.1 jit_solution(5593311353312125174)
XLA Ops:
  6.5 1.1 copy.30
  7.6 0.1 fusion.25
  7.8 9.9 %psum.14 = f32[1,512]{1,0:T(1,128)S(1)} all-reduce(f32[1,512]{1,0:T(1,128)S(1)} %bitcast.51), channel_id=1, replica_groups=mesh['rows'=8,'chan'=4] {'chan'}, use_global_device_ids=true, to_apply=%region_1.0 | all-reduce | flops 512 | bytes 4096 | tf_op jit(solution)/shard_map/psum | solution.py:39
  17.7 1.6 %multiply_convert_fusion.1 = bf16[256,1,512]{0,2,1:T(8,128)(2,1)} fusion(bf16[256,1,512]{0,2,1:T(8,128)(2,1)S(1)} %copy.30, f32[512]{0:T(512)S(1)} %bitcast.50, f32[256]{0:T(256)} %param.8), kind=kLoop, calls=%fused_computation.36 | loop fusion | flops 1048576 | bytes 527360 | tf_op jit(solution)/shard_map/convert_element_type | solution.py:41
  19.4 0.0 all-gather.3.cloned.1.call-update
  19.4 0.0 all-gather.5.cloned.1.call-start
  19.4 29.5 %all-gather.3.cloned.1.call-done = bf16[1024,1,512]{0,2,1:T(8,128)(2,1)} async-done(((bf16[256,1,512]{0,2,1:T(8,128)(2,1)}), bf16[1024,1,512]{0,2,1:T(8,128)(2,1)}) %all-gather.3.cloned.1.call-update) | async-done | bytes 1048592 | tf_op jit(solution)/shard_map/all_gather | solution.py:47
  49.0 1.0 fusion.37
  50.0 3.6 %collective-permute-start = (bf16[1024,1,64]{0,2,1:T(8,128)(2,1)S(1)}, bf16[1024,1,64]{0,2,1:T(8,128)(2,1)S(1)}, u32[]{:S(2)}, u32[]{:S(2)}) collective-permute-start(bf16[1024,1,64]{0,2,1:T(8,128)(2,1)S(1)} %get-tuple-element.7), channel_id=1, source_target_pairs={{0,4},{4,8},{8,12},{12,16},{16,20},{20,24},{24,28},{1,5},{5,9},{9,... | collective-permute-start | bytes 393224 | tf_op jit(solution)/shard_map/ppermute | solution.py:15
  53.6 1.9 %collective-permute-start.1 = (bf16[1024,1,64]{0,2,1:T(8,128)(2,1)S(1)}, bf16[1024,1,64]{0,2,1:T(8,128)(2,1)S(1)}, u32[]{:S(2)}, u32[]{:S(2)}) collective-permute-start(bf16[1024,1,64]{0,2,1:T(8,128)(2,1)S(1)} %get-tuple-element.8), channel_id=1, source_target_pairs={{4,0},{8,4},{12,8},{16,12},{20,16},{24,20},{28,24},{5,1},{9,5},{13... | collective-permute-start | bytes 393224 | tf_op jit(solution)/shard_map/ppermute | solution.py:18
  55.5 0.0 collective-permute-done
  55.6 5.2 %collective-permute-done.1 = bf16[1024,1,64]{0,2,1:T(8,128)(2,1)S(1)} collective-permute-done((bf16[1024,1,64]{0,2,1:T(8,128)(2,1)S(1)}, bf16[1024,1,64]{0,2,1:T(8,128)(2,1)S(1)}, u32[]{:S(2)}, u32[]{:S(2)}) %collective-permute-start.1) | collective-permute-done | bytes 131104 | tf_op jit(solution)/shard_map/ppermute | solution.py:18
  60.8 1.3 pad_maximum_fusion
  62.1 1.5 pad
  63.6 2.5 %reshape.158 = bf16[1024,1,10,1,8,9]{0,5,4,2,3,1:T(8,128)(2,1)S(1)} reshape(bf16[1024,1,10,1,72]{0,4,2,3,1:T(8,128)(2,1)} %pad) | data formatting | bytes 2949120 | tf_op jit(solution)/shard_map/conv_general_dilated | solution.py:27
  66.2 0.0 copy-start
  66.2 0.0 copy-start.3
  66.2 1.0 copy.32
  67.2 0.1 slice.23
  67.3 11.8 %add_multiply_fusion = (f32[1,8,8,9,256]{4,2,3,1,0:T(8,128)S(1)}, f32[1,8,8,9,256]{4,2,3,1,0:T(8,128)S(1)}) fusion(f32[256]{0:T(256)S(1)} %copy-done, bf16[3,3,3,256,1024]{4,3,2,1,0:T(8,128)(2,1)} %param.9, bf16[1024,1,10,1,7,2]{0,4,5,2,3,1:T(8,128)(2,1)S(1)} %slice.23, bf16[1024,1,10,1,8,9]{0,4,5,2,3,1:T(8,128)(2,1)S(1)} %copy.32, ...), kind=kOutput, calls=%fused_computation.24 | convolution fusion | flops 2723758080 | bytes 17097800 | tf_op jit(solution)/shard_map/conv_general_dilated | solution.py:27
  79.1 0.0 copy-start.1
  79.1 0.2 copy.35
  79.3 0.1 slice_reduce_fusion
  79.4 0.1 copy.36
  79.5 0.1 reduce_sum.25
  79.6 7.4 %psum.15 = f32[1,512]{1,0:T(1,128)S(1)} all-reduce(f32[1,512]{1,0:T(1,128)S(1)} %reduce_sum.25), channel_id=1, replica_groups=mesh['rows'=8,'chan'=4] {'chan'}, use_global_device_ids=true, to_apply=%region_3.4 | all-reduce | flops 512 | bytes 4096 | tf_op jit(solution)/shard_map/psum | solution.py:39
  87.0 0.2 copy.33
  87.2 0.2 copy.34
  87.4 1.0 multiply_convert_fusion
  88.4 0.0 all-gather.5.cloned.1.call-update
  88.4 27.1 %all-gather.5.cloned.1.call-done = bf16[1024,1,512]{0,2,1:T(8,128)(2,1)} async-done(((bf16[256,1,512]{0,2,1:T(8,128)(2,1)}), bf16[1024,1,512]{0,2,1:T(8,128)(2,1)}) %all-gather.5.cloned.1.call-update) | async-done | bytes 1048592 | tf_op jit(solution)/shard_map/all_gather | solution.py:47
  115.5 1.0 fusion.36
  116.5 3.6 %collective-permute-start.2 = (bf16[1024,1,64]{0,2,1:T(8,128)(2,1)S(1)}, bf16[1024,1,64]{0,2,1:T(8,128)(2,1)S(1)}, u32[]{:S(2)}, u32[]{:S(2)}) collective-permute-start(bf16[1024,1,64]{0,2,1:T(8,128)(2,1)S(1)} %get-tuple-element.5), channel_id=1, source_target_pairs={{0,4},{4,8},{8,12},{12,16},{16,20},{20,24},{24,28},{1,5},{5,9},{9,... | collective-permute-start | bytes 393224 | tf_op jit(solution)/shard_map/ppermute | solution.py:15
  120.1 2.1 %collective-permute-start.3 = (bf16[1024,1,64]{0,2,1:T(8,128)(2,1)S(1)}, bf16[1024,1,64]{0,2,1:T(8,128)(2,1)S(1)}, u32[]{:S(2)}, u32[]{:S(2)}) collective-permute-start(bf16[1024,1,64]{0,2,1:T(8,128)(2,1)S(1)} %get-tuple-element.6), channel_id=1, source_target_pairs={{4,0},{8,4},{12,8},{16,12},{20,16},{24,20},{28,24},{5,1},{9,5},{13... | collective-permute-start | bytes 393224 | tf_op jit(solution)/shard_map/ppermute | solution.py:18
  122.2 0.0 collective-permute-done.2
  122.2 5.1 %collective-permute-done.3 = bf16[1024,1,64]{0,2,1:T(8,128)(2,1)S(1)} collective-permute-done((bf16[1024,1,64]{0,2,1:T(8,128)(2,1)S(1)}, bf16[1024,1,64]{0,2,1:T(8,128)(2,1)S(1)}, u32[]{:S(2)}, u32[]{:S(2)}) %collective-permute-start.3) | collective-permute-done | bytes 131104 | tf_op jit(solution)/shard_map/ppermute | solution.py:18
  127.3 1.3 pad_maximum_fusion.1
  128.6 1.5 pad.2
  130.1 2.5 %reshape.167 = bf16[1024,1,10,1,8,9]{0,5,4,2,3,1:T(8,128)(2,1)S(1)} reshape(bf16[1024,1,10,1,72]{0,4,2,3,1:T(8,128)(2,1)} %pad.2) | data formatting | bytes 2949120 | tf_op jit(solution)/shard_map/conv_general_dilated | solution.py:27
  132.7 1.0 copy.38
  133.6 0.1 slice.28
  133.7 11.9 %fusion.16 = f32[1,8,8,9,256]{4,2,3,1,0:T(8,128)S(1)} fusion(bf16[3,3,3,256,1024]{4,3,2,1,0:T(8,128)(2,1)} %param.12, bf16[1024,1,10,1,7,2]{0,4,5,2,3,1:T(8,128)(2,1)S(1)} %slice.28, bf16[1024,1,10,1,8,9]{0,4,5,2,3,1:T(8,128)(2,1)S(1)} %copy.38, pred[8,9]{0,1:T(8,128)(4,1)S(1)} %copy-done.3), kind=kOutput, calls=%fused_computation.17 | convolution fusion | flops 2723463168 | bytes 16506952 | tf_op jit(solution)/shard_map/conv_general_dilated | solution.py:27
  145.6 0.0 copy-start.2
  145.6 0.2 copy.39
  145.9 0.2 copy.40
  146.1 0.2 copy-done.2
  146.3 0.1 fusion.27
  146.4 0.8 copy.41
  (8 shorter events, 0.1 us)
Async XLA Ops:
  6.5 42.4 %all-gather.3.cloned.1.call-start = ((), (), s32[]{:S(2)}) async-start(), calls=%async_computation | async-start | bytes 1310720 | tf_op jit(solution)/shard_map/all_gather | solution.py:47
  19.4 96.1 %all-gather.5.cloned.1.call-start = ((), (), s32[]{:S(2)}) async-start(), calls=%async_computation.1 | async-start | bytes 1310720 | tf_op jit(solution)/shard_map/all_gather | solution.py:47
  50.0 5.6 %collective-permute-start = (bf16[1024,1,64]{0,2,1:T(8,128)(2,1)S(1)}, bf16[1024,1,64]{0,2,1:T(8,128)(2,1)S(1)}, u32[]{:S(2)}, u32[]{:S(2)}) collective-permute-start(bf16[1024,1,64]{0,2,1:T(8,128)(2,1)S(1)} %get-tuple-element.7), channel_id=1, source_target_pairs={{0,4},{4,8},{8,12},{12,16},{16,20},{20,24},{24,28},{1,5},{5,9},{9,... | collective-permute-start | bytes 393224 | tf_op jit(solution)/shard_map/ppermute | solution.py:15
  53.6 7.2 %collective-permute-start.1 = (bf16[1024,1,64]{0,2,1:T(8,128)(2,1)S(1)}, bf16[1024,1,64]{0,2,1:T(8,128)(2,1)S(1)}, u32[]{:S(2)}, u32[]{:S(2)}) collective-permute-start(bf16[1024,1,64]{0,2,1:T(8,128)(2,1)S(1)} %get-tuple-element.8), channel_id=1, source_target_pairs={{4,0},{8,4},{12,8},{16,12},{20,16},{24,20},{28,24},{5,1},{9,5},{13... | collective-permute-start | bytes 393224 | tf_op jit(solution)/shard_map/ppermute | solution.py:18
  66.2 1.1 copy-start
  66.2 1.1 copy-start.3
  79.1 8.3 %copy-start.1 = (f32[256]{0:T(256)S(1)}, f32[256]{0:T(256)}, u32[]{:S(2)}) copy-start(f32[256]{0:T(256)} %param.11) | copy-start | bytes 3076
  116.5 5.8 %collective-permute-start.2 = (bf16[1024,1,64]{0,2,1:T(8,128)(2,1)S(1)}, bf16[1024,1,64]{0,2,1:T(8,128)(2,1)S(1)}, u32[]{:S(2)}, u32[]{:S(2)}) collective-permute-start(bf16[1024,1,64]{0,2,1:T(8,128)(2,1)S(1)} %get-tuple-element.5), channel_id=1, source_target_pairs={{0,4},{4,8},{8,12},{12,16},{16,20},{20,24},{24,28},{1,5},{5,9},{9,... | collective-permute-start | bytes 393224 | tf_op jit(solution)/shard_map/ppermute | solution.py:15
  120.1 7.2 %collective-permute-start.3 = (bf16[1024,1,64]{0,2,1:T(8,128)(2,1)S(1)}, bf16[1024,1,64]{0,2,1:T(8,128)(2,1)S(1)}, u32[]{:S(2)}, u32[]{:S(2)}) collective-permute-start(bf16[1024,1,64]{0,2,1:T(8,128)(2,1)S(1)} %get-tuple-element.6), channel_id=1, source_target_pairs={{4,0},{8,4},{12,8},{16,12},{20,16},{24,20},{28,24},{5,1},{9,5},{13... | collective-permute-start | bytes 393224 | tf_op jit(solution)/shard_map/ppermute | solution.py:18
  145.6 0.7 copy-start.2
Sparse Core Ops, SparseCore 0:
  19.5 29.4 all-gather.2
  88.5 26.9 all-gather.4
where the time goes:
time: 155 us; the launch traced here: 154 us
  waiting for transfers between devices  67 us (43%)
  matrix products  23.7 us (15%)
  blocking collectives  17.4 us (11%)
  local copies, waits for them, and re-layouts  15.4 us (10%)
  between operations  13.7 us (9%)
  starting transfers between devices  11.3 us (7%)
  other arithmetic  5.62 us (4%)
    all_gather x2, waiting for transfers between devices, convolve(): whole = lax.all_gather(block, 'chan', axis=0, tiled=True)  56.6 us
    conv_general_dilated x2, matrix products, conv_rows(): lax.conv_general_dilated(grid, kernel, (1, 1, 1), ((2, 0), (0, 0), (1, 1)...  23.7 us
    psum x2, blocking collectives, activate(): totals = lax.psum(jnp.sum(values * values, axis=0), 'chan')  17.4 us
    ppermute x2, waiting for transfers between devices, padded(): lax.ppermute(lax.slice_in_dim(block, 0, width, axis=dim), axis, backward)  10.3 us
    conv_general_dilated x12, local copies, waits for them, and re-layouts, conv_rows(): lax.conv_general_dilated(grid, kernel, (1, 1, 1), ((2, 0), (0, 0), (1, 1)...  7.92 us
    ppermute x2, starting transfers between devices, padded(): lax.ppermute(lax.slice_in_dim(block, block.shape[dim] - width, None, axis...  7.28 us
    ppermute x2, starting transfers between devices, padded(): lax.ppermute(lax.slice_in_dim(block, 0, width, axis=dim), axis, backward)  4.02 us
  transfers between devices with their start and end apart: 6, of which 4 were waited for; matrix products, arithmetic and copies ran while one was open for 0% of the time, Pallas kernels for 0%

commit v1 on v0

v1 whole, which is shorter than its diff:
```python
import jax
import jax.numpy as jnp
from jax import lax
from jax.experimental import pallas as pl
from jax.experimental.pallas import tpu as pltpu
from jax.sharding import PartitionSpec as P

WIDTH = 64
LANES = 128


def shift_along(block, axis, step):
    count = lax.axis_size(axis)
    pairs = [(i, i + step) for i in range(count) if 0 <= i + step < count]
    return lax.ppermute(block, axis, pairs)


def ring(block, axis, step=1):
    count = lax.axis_size(axis)
    return lax.ppermute(block, axis, [(i, (i + step) % count) for i in range(count)])


def ring_gather(block, axis):
    blocks = [block]
    for _ in range(lax.axis_size(axis) - 1):
        blocks.append(ring(blocks[-1], axis))
    return blocks


def conv_kernel(count, frame, residual, *refs):
    place = refs[0]
    edges = refs[1 : 1 + count]
    inner = refs[1 + count : 1 + 2 * count]
    above, above_last, below, below_last, gains, bias, weights = refs[1 + 2 * count : 8 + 2 * count]
    rest = refs[8 + 2 * count :]
    if residual:
        source, out, taps, acts, sums, sems = rest
    else:
        out, taps, acts, sums, sems = rest
    copies = [
        pltpu.make_async_copy(weights.at[frame, q, s], taps.at[q * 3 + s], sems.at[q * 3 + s])
        for q in range(3)
        for s in range(3)
    ]
    for copy in copies:
        copy.start()
    width = edges[0].shape[1]
    cells = acts.shape[1] - 2 * WIDTH
    total = acts.shape[2]

    def parts(r):
        top = above[r] if r < count - 1 else above_last[...]
        low = below[r] if r < count - 1 else below_last[...]
        return jnp.concatenate(
            [top, edges[r][:WIDTH], inner[r][...], edges[r][WIDTH:], low], axis=0
        ).astype(jnp.float32)

    squares = jnp.zeros((cells + 2 * WIDTH, 1), jnp.float32)
    for r in range(count):
        values = parts(r)
        squares += jnp.sum(values * values, axis=1, keepdims=True)
    sums[...] = lax.rsqrt(squares / total + 1e-6)
    column = lax.broadcasted_iota(jnp.int32, (cells + 2 * WIDTH, width), 0) % WIDTH
    for r in range(count):
        owner = lax.rem(place[0] + count - r, count)
        lanes = pl.ds(pl.multiple_of(owner * width, width), width)
        scaled = parts(r) * gains[r : r + 1, :] * sums[...]
        value = scaled / (1.0 + jnp.exp(-scaled))
        acts[1, :, lanes] = value.astype(jnp.bfloat16)
        before = jnp.where(column == 0, 0.0, pltpu.roll(value, 1, 0))
        acts[0, :, lanes] = before.astype(jnp.bfloat16)
        after = jnp.where(column == WIDTH - 1, 0.0, pltpu.roll(value, value.shape[0] - 1, 0))
        acts[2, :, lanes] = after.astype(jnp.bfloat16)
    result = jnp.broadcast_to(bias[...], (cells, bias.shape[1]))
    for q in range(3):
        for s in range(3):
            copies[q * 3 + s].wait()
            result += lax.dot_general(
                acts[s, q * WIDTH : q * WIDTH + cells, :],
                taps[q * 3 + s],
                (((1,), (1,)), ((), ())),
                preferred_element_type=jnp.float32,
            )
    if residual:
        result = result + source[...].astype(jnp.float32)
        out[...] = result.T.astype(out.dtype)
    else:
        out[...] = result.astype(out.dtype)


def conv_stage(block, gains, bias, weights, source=None):
    count = lax.axis_size("chan")
    cells, width = block.shape
    edges = ring_gather(jnp.concatenate([block[:WIDTH], block[cells - WIDTH :]], axis=0), "chan")
    inner = ring_gather(block[WIDTH : cells - WIDTH], "chan")
    above = shift_along(jnp.stack([e[WIDTH:] for e in edges[:-1]]), "rows", 1)
    below = shift_along(jnp.stack([e[:WIDTH] for e in edges[:-1]]), "rows", -1)
    above_last = shift_along(edges[-1][WIDTH:], "rows", 1)
    below_last = shift_along(edges[-1][:WIDTH], "rows", -1)
    outs = weights.shape[3]
    operands = [
        lax.axis_index("chan").astype(jnp.int32).reshape(1),
        *edges,
        *inner,
        above,
        above_last,
        below,
        below_last,
        gains,
        bias.reshape(1, outs),
        weights,
    ]
    if source is not None:
        operands.append(source)
    vmem = pl.BlockSpec(memory_space=pltpu.VMEM)
    in_specs = [pl.BlockSpec(memory_space=pltpu.SMEM)] + [vmem] * (len(operands) - 1)
    in_specs[7 + 2 * count] = pl.BlockSpec(memory_space=pl.ANY)
    total = width * count
    shape = (cells, outs) if source is None else (outs, cells)

    def kernel(*refs):
        conv_kernel(count, weights.shape[0] - 1, source is not None, *refs)

    return pl.pallas_call(
        kernel,
        out_shape=jax.ShapeDtypeStruct(shape, jnp.bfloat16),
        in_specs=in_specs,
        out_specs=vmem,
        scratch_shapes=[
            pltpu.VMEM((9, outs, total), jnp.bfloat16),
            pltpu.VMEM((3, cells + 2 * WIDTH, total), jnp.bfloat16),
            pltpu.VMEM((cells + 2 * WIDTH, 1), jnp.float32),
            pltpu.SemaphoreType.DMA((9,)),
        ],
        compiler_params=pltpu.CompilerParams(vmem_limit_bytes=40 << 20),
    )(*operands)


def padded(block, width):
    low = shift_along(block[..., block.shape[-1] - width :], "rows", 1)
    high = shift_along(block[..., :width], "rows", -1)
    return jnp.concatenate([low, block, high], axis=-1)


def activate(values, gain, total):
    mean_sq = lax.psum(jnp.sum(values * values, axis=0, keepdims=True), "chan") / total
    return jax.nn.silu(values * gain[:, None, None] / jnp.sqrt(mean_sq + 1e-06)).astype(jnp.bfloat16)


def convolve(block, kernel):
    whole = padded(lax.all_gather(block, "chan", axis=0, tiled=True), WIDTH)
    channels, frames, cells = whole.shape
    grid = whole.reshape(1, channels, frames, cells // WIDTH, WIDTH)
    result = lax.conv_general_dilated(
        grid,
        kernel,
        (1, 1, 1),
        ((2, 0), (0, 0), (1, 1)),
        dimension_numbers=("NCDHW", "DHWOI", "NCDHW"),
        preferred_element_type=jnp.float32,
    )
    return result[0].reshape(kernel.shape[3], frames, cells - 2 * WIDTH)


def general(features, gain_first, weight_first, bias_first, gain_second, weight_second, bias_second):
    total = weight_first.shape[4]
    source = features.astype(jnp.float32)
    middle = convolve(activate(source, gain_first, total), weight_first) + bias_first[:, None, None]
    result = convolve(activate(middle, gain_second, total), weight_second)
    return (source + result + bias_second[:, None, None]).astype(jnp.bfloat16)


def on_device(
    features, gain_first, weight_first, bias_first, gain_second, weight_second, bias_second
):
    channels, frames, cells = features.shape
    if frames != 1 or channels % LANES or cells < 3 * WIDTH:
        return general(
            features, gain_first, weight_first, bias_first, gain_second, weight_second, bias_second
        )
    block = features.reshape(channels, cells).T
    count = lax.axis_size("chan")
    pair = jnp.stack([gain_first, gain_second])
    pairs = jnp.stack([pair] + [ring(pair, "chan", r) for r in range(1, count)])
    middle = conv_stage(block, pairs[:, 0], bias_first, weight_first)
    out = conv_stage(middle, pairs[:, 1], bias_second, weight_second, block)
    return out.reshape(channels, frames, cells)


def solution(mesh):
    in_specs = (
        P("chan", None, "rows"),
        P("chan"),
        P(None, None, None, "chan", None),
        P("chan"),
        P("chan"),
        P(None, None, None, "chan", None),
        P("chan"),
    )
    return jax.shard_map(
        on_device, mesh=mesh, in_specs=in_specs, out_specs=P("chan", None, "rows"), check_vma=False
    )
```

time: 155 us -> 94.5 us (0.61)
  waiting for transfers between devices: 67 us -> 37.8 us
  matrix products: 23.7 us -> 0 us
  starting transfers between devices: 11.3 us -> 34.3 us
  Pallas kernels: 0 us -> 17.6 us
  blocking collectives: 17.4 us -> 0 us
  local copies, waits for them, and re-layouts: 15.4 us -> 1.86 us
  between operations: 13.7 us -> 0.38 us
  other arithmetic: 5.62 us -> 0.8 us
    all_gather x2 -> x0, waiting for transfers between devices: 56.6 us -> none  [convolve(): whole = lax.all_gather(block, 'chan', axis=0, tiled=True)]
    ppermute x4 -> x23, waiting for transfers between devices: 10.3 us -> 37.8 us  [the longest x15 35.8 us: ring(): lax.ppermute(block, axis, [(i, (i + step) % count) for i in range(count)])]
    conv_general_dilated x2 -> x0, matrix products: 23.7 us -> none  [conv_rows(): lax.conv_general_dilated(grid, kernel, (1, 1, 1), ((2, 0), (0, 0), (1, 1)...]
    ppermute x4 -> x23, starting transfers between devices: 11.3 us -> 34.3 us  [the longest x8 27.9 us: shift_along(): return lax.ppermute(block, axis, pairs)]
    pallas_call x0 -> x2, Pallas kernels: none -> 17.6 us  [conv_stage(): pl.pallas_call(kernel, out_shape=jax.ShapeDtypeStruct(shape, jnp.bfloat16...]
    psum x2 -> x0, blocking collectives: 17.4 us -> none  [activate(): totals = lax.psum(jnp.sum(values * values, axis=0), 'chan')]
    conv_general_dilated x12 -> x0, local copies, waits for them, and re-layouts: 7.92 us -> none  [conv_rows(): lax.conv_general_dilated(grid, kernel, (1, 1, 1), ((2, 0), (0, 0), (1, 1)...]
    reshape x2 -> x0, local copies, waits for them, and re-layouts: 3.02 us -> none  [conv_rows(): grid = data.reshape(1, channels, frames, rows_in, WIDTH)]
  transfers between devices with their start and end apart: 6 -> 23, of which waited for: 4 -> 9; matrix products, arithmetic and copies ran while one was open for 0% -> 1% of each run, Pallas kernels for 0% -> 0%
where the time goes in v1:
time: 94.5 us; the launch traced here: 92.7 us
  waiting for transfers between devices  37.8 us (40%)
  starting transfers between devices  34.3 us (36%)
  Pallas kernels  17.6 us (19%)
  local copies, waits for them, and re-layouts  1.86 us (2%)
    ppermute x15, waiting for transfers between devices, ring(): lax.ppermute(block, axis, [(i, (i + step) % count) for i in range(count)])  35.8 us
    ppermute x8, starting transfers between devices, shift_along(): return lax.ppermute(block, axis, pairs)  27.9 us
    pallas_call x2, Pallas kernels, conv_stage(): pl.pallas_call(kernel, out_shape=jax.ShapeDtypeStruct(shape, jnp.bfloat16...  17.6 us
    ppermute x15, starting transfers between devices, ring(): lax.ppermute(block, axis, [(i, (i + step) % count) for i in range(count)])  6.43 us
    ppermute x8, waiting for transfers between devices, shift_along(): return lax.ppermute(block, axis, pairs)  1.91 us
  transfers between devices with their start and end apart: 23, of which 9 were waited for; matrix products, arithmetic and copies ran while one was open for 1% of the time, Pallas kernels for 0%

profile of v1, /device:TPU:3, one launch (start us, length us, event | category | flops | bytes accessed | tf_op | source)
XLA Modules:
  0.0 92.7 jit_solution(16445749720334336198)
XLA Ops:
  0.0 0.7 fusion
  0.7 2.3 %collective-permute-start.11 = (f32[2,256]{1,0:T(2,128)S(1)}, f32[2,256]{1,0:T(2,128)S(1)}, u32[]{:S(2)}, u32[]{:S(2)}) collective-permute-start(f32[2,256]{1,0:T(2,128)S(1)} %get-tuple-element.28), channel_id=1, source_target_pairs={{0,2},{1,3},{2,0},{3,1},{4,6},{5,7},{6,4},{7,5},{8,10},{9,11},{10,... | collective-permute-start | bytes 6152 | tf_op jit(solution)/shard_map/ppermute | solution.py:20
  3.0 1.3 %collective-permute-start.10 = (f32[2,256]{1,0:T(2,128)S(1)}, f32[2,256]{1,0:T(2,128)S(1)}, u32[]{:S(2)}, u32[]{:S(2)}) collective-permute-start(f32[2,256]{1,0:T(2,128)S(1)} %get-tuple-element.28), channel_id=1, source_target_pairs={{0,1},{1,2},{2,3},{3,0},{4,5},{5,6},{6,7},{7,4},{8,9},{9,10},{10,1... | collective-permute-start | bytes 6152 | tf_op jit(solution)/shard_map/ppermute | solution.py:20
  4.3 2.0 %collective-permute-start.12 = (f32[2,256]{1,0:T(2,128)S(1)}, f32[2,256]{1,0:T(2,128)S(1)}, u32[]{:S(2)}, u32[]{:S(2)}) collective-permute-start(f32[2,256]{1,0:T(2,128)S(1)} %get-tuple-element.28), channel_id=1, source_target_pairs={{0,3},{1,0},{2,1},{3,2},{4,7},{5,4},{6,5},{7,6},{8,11},{9,8},{10,9... | collective-permute-start | bytes 6152 | tf_op jit(solution)/shard_map/ppermute | solution.py:20
  6.3 1.1 %copy.8 = bf16[256,1,512]{0,2,1:T(8,128)(2,1)S(1)} copy(bf16[256,1,512]{2,0,1:T(8,128)(2,1)} %param.7) | data formatting | bytes 524288 | tf_op args[0]
  7.4 0.1 collective-permute-start
  7.5 0.1 collective-permute-start.3
  7.6 0.0 collective-permute-done.11
  7.6 0.0 collective-permute-done.10
  7.6 0.0 collective-permute-done.12
  7.7 4.7 %collective-permute-done.refs_2_ = bf16[128,256]{1,0:T(8,128)(2,1)S(1)} collective-permute-done((bf16[128,256]{1,0:T(8,128)(2,1)S(1)}, bf16[128,256]{1,0:T(8,128)(2,1)S(1)}, u32[]{:S(2)}, u32[]{:S(2)}) %collective-permute-start) | collective-permute-done | bytes 65568 | tf_op jit(solution)/shard_map/ppermute | solution.py:20
  12.4 0.0 collective-permute-start.1
  12.4 5.9 %collective-permute-done.1.refs_3_ = bf16[128,256]{1,0:T(8,128)(2,1)S(1)} collective-permute-done((bf16[128,256]{1,0:T(8,128)(2,1)S(1)}, bf16[128,256]{1,0:T(8,128)(2,1)S(1)}, u32[]{:S(2)}, u32[]{:S(2)}) %collective-permute-start.1) | collective-permute-done | bytes 65568 | tf_op jit(solution)/shard_map/ppermute | solution.py:20
  18.3 6.5 %collective-permute-start.6 = (bf16[3,64,256]{2,1,0:T(8,128)(2,1)S(1)}, bf16[3,64,256]{2,1,0:T(8,128)(2,1)S(1)}, u32[]{:S(2)}, u32[]{:S(2)}) collective-permute-start(bf16[3,64,256]{2,1,0:T(8,128)(2,1)S(1)} %pad_maximum_fusion), channel_id=1, source_target_pairs={{0,4},{4,8},{8,12},{12,16},{16,20},{20,24},{24,28},{1,5},{5,9},{9,... | collective-permute-start | bytes 294920 | tf_op jit(solution)/shard_map/ppermute | solution.py:15
  24.8 0.1 collective-permute-start.2
  24.9 1.9 %collective-permute-start.8 = (bf16[3,64,256]{2,1,0:T(8,128)(2,1)S(1)}, bf16[3,64,256]{2,1,0:T(8,128)(2,1)S(1)}, u32[]{:S(2)}, u32[]{:S(2)}) collective-permute-start(bf16[3,64,256]{2,1,0:T(8,128)(2,1)S(1)} %pad_maximum_fusion.1), channel_id=1, source_target_pairs={{4,0},{8,4},{12,8},{16,12},{20,16},{24,20},{28,24},{5,1},{9,5},{13... | collective-permute-start | bytes 294920 | tf_op jit(solution)/shard_map/ppermute | solution.py:15
  26.9 0.0 collective-permute-done.3.refs_6_
  26.9 0.1 collective-permute-start.4
  26.9 3.0 %collective-permute-done.2.refs_4_ = bf16[128,256]{1,0:T(8,128)(2,1)S(1)} collective-permute-done((bf16[128,256]{1,0:T(8,128)(2,1)S(1)}, bf16[128,256]{1,0:T(8,128)(2,1)S(1)}, u32[]{:S(2)}, u32[]{:S(2)}) %collective-permute-start.2) | collective-permute-done | bytes 65568 | tf_op jit(solution)/shard_map/ppermute | solution.py:20
  29.9 2.0 %collective-permute-start.9 = (bf16[64,256]{1,0:T(8,128)(2,1)S(1)}, bf16[64,256]{1,0:T(8,128)(2,1)S(1)}, u32[]{:S(2)}, u32[]{:S(2)}) collective-permute-start(bf16[64,256]{1,0:T(8,128)(2,1)S(1)} %get-tuple-element.19), channel_id=1, source_target_pairs={{4,0},{8,4},{12,8},{16,12},{20,16},{24,20},{28,24},{5,1},{9,5},{13... | collective-permute-start | bytes 98312 | tf_op jit(solution)/shard_map/ppermute | solution.py:15
  31.9 4.5 %collective-permute-start.7 = (bf16[64,256]{1,0:T(8,128)(2,1)S(1)}, bf16[64,256]{1,0:T(8,128)(2,1)S(1)}, u32[]{:S(2)}, u32[]{:S(2)}) collective-permute-start(bf16[64,256]{1,0:T(8,128)(2,1)S(1)} %get-tuple-element.20), channel_id=1, source_target_pairs={{0,4},{4,8},{8,12},{12,16},{16,20},{20,24},{24,28},{1,5},{5,9},{9,... | collective-permute-start | bytes 98312 | tf_op jit(solution)/shard_map/ppermute | solution.py:15
  36.4 0.0 collective-permute-done.4.refs_7_
  36.4 0.1 collective-permute-start.5
  36.5 0.0 collective-permute-done.9.refs_12_
  36.5 0.9 collective-permute-done.7.refs_10_
  37.4 0.0 collective-permute-done.6.refs_9_
  37.4 7.7 %collective-permute-done.5.refs_8_ = bf16[384,256]{1,0:T(8,128)(2,1)S(1)} collective-permute-done((bf16[384,256]{1,0:T(8,128)(2,1)S(1)}, bf16[384,256]{1,0:T(8,128)(2,1)S(1)}, u32[]{:S(2)}, u32[]{:S(2)}) %collective-permute-start.5) | collective-permute-done | bytes 196640 | tf_op jit(solution)/shard_map/ppermute | solution.py:20
  45.1 0.7 copy-done
  45.8 8.4 %shard_map.73 = bf16[512,256]{1,0:T(8,128)(2,1)S(1)} custom-call(s32[1]{0:T(128)} %bitcast.refs_0_, bf16[128,256]{1,0:T(8,128)(2,1)S(1)} %pad_maximum_fusion.4.refs_1_, bf16[128,256]{1,0:T(8,128)(2,1)S(1)} %collective-permute-done.refs_2_, bf16[128,256]{1,0:T(8,128)(2,1)S(1)} %collective-permute-done.1.refs_3_, ...), custom_call_target="tpu_custom_call" | custom-call | tf_op jit(solution)/shard_map/pallas_call | solution.py:124
  54.2 0.1 collective-permute-start.13
  54.3 0.1 collective-permute-start.16
  54.4 4.8 %collective-permute-done.13.refs_2_ = bf16[128,256]{1,0:T(8,128)(2,1)S(1)} collective-permute-done((bf16[128,256]{1,0:T(8,128)(2,1)S(1)}, bf16[128,256]{1,0:T(8,128)(2,1)S(1)}, u32[]{:S(2)}, u32[]{:S(2)}) %collective-permute-start.13) | collective-permute-done | bytes 65568 | tf_op jit(solution)/shard_map/ppermute | solution.py:20
  59.2 0.0 collective-permute-start.14
  59.2 5.9 %collective-permute-done.14.refs_3_ = bf16[128,256]{1,0:T(8,128)(2,1)S(1)} collective-permute-done((bf16[128,256]{1,0:T(8,128)(2,1)S(1)}, bf16[128,256]{1,0:T(8,128)(2,1)S(1)}, u32[]{:S(2)}, u32[]{:S(2)}) %collective-permute-start.14) | collective-permute-done | bytes 65568 | tf_op jit(solution)/shard_map/ppermute | solution.py:20
  65.1 0.0 collective-permute-done.16.refs_6_
  65.1 0.1 collective-permute-start.17
  65.2 4.6 %collective-permute-start.19 = (bf16[3,64,256]{2,1,0:T(8,128)(2,1)S(1)}, bf16[3,64,256]{2,1,0:T(8,128)(2,1)S(1)}, u32[]{:S(2)}, u32[]{:S(2)}) collective-permute-start(bf16[3,64,256]{2,1,0:T(8,128)(2,1)S(1)} %pad_maximum_fusion.2), channel_id=1, source_target_pairs={{0,4},{4,8},{8,12},{12,16},{16,20},{20,24},{24,28},{1,5},{5,9},{9,... | collective-permute-start | bytes 294920 | tf_op jit(solution)/shard_map/ppermute | solution.py:15
  69.8 0.1 collective-permute-start.15
  69.9 1.9 %collective-permute-start.21 = (bf16[3,64,256]{2,1,0:T(8,128)(2,1)S(1)}, bf16[3,64,256]{2,1,0:T(8,128)(2,1)S(1)}, u32[]{:S(2)}, u32[]{:S(2)}) collective-permute-start(bf16[3,64,256]{2,1,0:T(8,128)(2,1)S(1)} %pad_maximum_fusion.3), channel_id=1, source_target_pairs={{4,0},{8,4},{12,8},{16,12},{20,16},{24,20},{28,24},{5,1},{9,5},{13... | collective-permute-start | bytes 294920 | tf_op jit(solution)/shard_map/ppermute | solution.py:15
  71.8 0.0 collective-permute-done.17.refs_7_
  71.8 0.3 collective-permute-start.18
  72.1 3.9 %collective-permute-done.15.refs_4_ = bf16[128,256]{1,0:T(8,128)(2,1)S(1)} collective-permute-done((bf16[128,256]{1,0:T(8,128)(2,1)S(1)}, bf16[128,256]{1,0:T(8,128)(2,1)S(1)}, u32[]{:S(2)}, u32[]{:S(2)}) %collective-permute-start.15) | collective-permute-done | bytes 65568 | tf_op jit(solution)/shard_map/ppermute | solution.py:20
  76.0 2.4 %collective-permute-start.22 = (bf16[64,256]{1,0:T(8,128)(2,1)S(1)}, bf16[64,256]{1,0:T(8,128)(2,1)S(1)}, u32[]{:S(2)}, u32[]{:S(2)}) collective-permute-start(bf16[64,256]{1,0:T(8,128)(2,1)S(1)} %get-tuple-element.13), channel_id=1, source_target_pairs={{4,0},{8,4},{12,8},{16,12},{20,16},{24,20},{28,24},{5,1},{9,5},{13... | collective-permute-start | bytes 98312 | tf_op jit(solution)/shard_map/ppermute | solution.py:15
  78.4 4.1 %collective-permute-start.20 = (bf16[64,256]{1,0:T(8,128)(2,1)S(1)}, bf16[64,256]{1,0:T(8,128)(2,1)S(1)}, u32[]{:S(2)}, u32[]{:S(2)}) collective-permute-start(bf16[64,256]{1,0:T(8,128)(2,1)S(1)} %get-tuple-element.14), channel_id=1, source_target_pairs={{0,4},{4,8},{8,12},{12,16},{16,20},{20,24},{24,28},{1,5},{5,9},{9,... | collective-permute-start | bytes 98312 | tf_op jit(solution)/shard_map/ppermute | solution.py:15
  82.5 0.0 collective-permute-done.22.refs_12_
  82.5 1.0 %collective-permute-done.20.refs_10_ = bf16[64,256]{1,0:T(8,128)(2,1)S(1)} collective-permute-done((bf16[64,256]{1,0:T(8,128)(2,1)S(1)}, bf16[64,256]{1,0:T(8,128)(2,1)S(1)}, u32[]{:S(2)}, u32[]{:S(2)}) %collective-permute-start.20) | collective-permute-done | bytes 32800 | tf_op jit(solution)/shard_map/ppermute | solution.py:15
  83.5 0.0 collective-permute-done.19.refs_9_
  83.5 9.2 %shard_map.74 = bf16[256,512]{1,0:T(8,128)(2,1)} custom-call(s32[1]{0:T(128)} %bitcast.refs_0_, bf16[128,256]{1,0:T(8,128)(2,1)S(1)} %pad_maximum_fusion.5.refs_1_, bf16[128,256]{1,0:T(8,128)(2,1)S(1)} %collective-permute-done.13.refs_2_, bf16[128,256]{1,0:T(8,128)(2,1)S(1)} %collective-permute-done.14.refs_3_, ...), custom_call_target="tpu_custom_call" | custom-call | tf_op jit(solution)/shard_map/pallas_call | solution.py:124
  (28 shorter events, 0.2 us)
Async XLA Ops:
  0.0 83.5 %copy-start.1 = (f32[256]{0:T(256)S(1)}, f32[256]{0:T(256)}, u32[]{:S(2)}) copy-start(f32[256]{0:T(256)} %param.13) | copy-start | bytes 3076
  0.7 6.9 %collective-permute-start.11 = (f32[2,256]{1,0:T(2,128)S(1)}, f32[2,256]{1,0:T(2,128)S(1)}, u32[]{:S(2)}, u32[]{:S(2)}) collective-permute-start(f32[2,256]{1,0:T(2,128)S(1)} %get-tuple-element.28), channel_id=1, source_target_pairs={{0,2},{1,3},{2,0},{3,1},{4,6},{5,7},{6,4},{7,5},{8,10},{9,11},{10,... | collective-permute-start | bytes 6152 | tf_op jit(solution)/shard_map/ppermute | solution.py:20
  3.0 4.6 %collective-permute-start.10 = (f32[2,256]{1,0:T(2,128)S(1)}, f32[2,256]{1,0:T(2,128)S(1)}, u32[]{:S(2)}, u32[]{:S(2)}) collective-permute-start(f32[2,256]{1,0:T(2,128)S(1)} %get-tuple-element.28), channel_id=1, source_target_pairs={{0,1},{1,2},{2,3},{3,0},{4,5},{5,6},{6,7},{7,4},{8,9},{9,10},{10,1... | collective-permute-start | bytes 6152 | tf_op jit(solution)/shard_map/ppermute | solution.py:20
  4.3 3.3 %collective-permute-start.12 = (f32[2,256]{1,0:T(2,128)S(1)}, f32[2,256]{1,0:T(2,128)S(1)}, u32[]{:S(2)}, u32[]{:S(2)}) collective-permute-start(f32[2,256]{1,0:T(2,128)S(1)} %get-tuple-element.28), channel_id=1, source_target_pairs={{0,3},{1,0},{2,1},{3,2},{4,7},{5,4},{6,5},{7,6},{8,11},{9,8},{10,9... | collective-permute-start | bytes 6152 | tf_op jit(solution)/shard_map/ppermute | solution.py:20
  7.4 5.0 %collective-permute-start = (bf16[128,256]{1,0:T(8,128)(2,1)S(1)}, bf16[128,256]{1,0:T(8,128)(2,1)S(1)}, u32[]{:S(2)}, u32[]{:S(2)}) collective-permute-start(bf16[128,256]{1,0:T(8,128)(2,1)S(1)} %pad_maximum_fusion.4.refs_1_), channel_id=1, source_target_pairs={{0,1},{1,2},{2,3},{3,0},{4,5},{5,6},{6,7},{7,4},{8,9},{9,10},{10,1... | collective-permute-start | bytes 196616 | tf_op jit(solution)/shard_map/ppermute | solution.py:20
  7.5 19.4 %collective-permute-start.3 = (bf16[384,256]{1,0:T(8,128)(2,1)S(1)}, bf16[384,256]{1,0:T(8,128)(2,1)S(1)}, u32[]{:S(2)}, u32[]{:S(2)}) collective-permute-start(bf16[384,256]{1,0:T(8,128)(2,1)S(1)} %slice.82.refs_5_), channel_id=1, source_target_pairs={{0,1},{1,2},{2,3},{3,0},{4,5},{5,6},{6,7},{7,4},{8,9},{9,10},{10,1... | collective-permute-start | bytes 589832 | tf_op jit(solution)/shard_map/ppermute | solution.py:20
  12.4 5.9 %collective-permute-start.1 = (bf16[128,256]{1,0:T(8,128)(2,1)S(1)}, bf16[128,256]{1,0:T(8,128)(2,1)S(1)}, u32[]{:S(2)}, u32[]{:S(2)}) collective-permute-start(bf16[128,256]{1,0:T(8,128)(2,1)S(1)} %collective-permute-done.refs_2_), channel_id=1, source_target_pairs={{0,1},{1,2},{2,3},{3,0},{4,5},{5,6},{6,7},{7,4},{8,9},{9,10},{10,1... | collective-permute-start | bytes 196616 | tf_op jit(solution)/shard_map/ppermute | solution.py:20
  18.3 19.1 %collective-permute-start.6 = (bf16[3,64,256]{2,1,0:T(8,128)(2,1)S(1)}, bf16[3,64,256]{2,1,0:T(8,128)(2,1)S(1)}, u32[]{:S(2)}, u32[]{:S(2)}) collective-permute-start(bf16[3,64,256]{2,1,0:T(8,128)(2,1)S(1)} %pad_maximum_fusion), channel_id=1, source_target_pairs={{0,4},{4,8},{8,12},{12,16},{16,20},{20,24},{24,28},{1,5},{5,9},{9,... | collective-permute-start | bytes 294920 | tf_op jit(solution)/shard_map/ppermute | solution.py:15
  24.8 5.0 %collective-permute-start.2 = (bf16[128,256]{1,0:T(8,128)(2,1)S(1)}, bf16[128,256]{1,0:T(8,128)(2,1)S(1)}, u32[]{:S(2)}, u32[]{:S(2)}) collective-permute-start(bf16[128,256]{1,0:T(8,128)(2,1)S(1)} %collective-permute-done.1.refs_3_), channel_id=1, source_target_pairs={{0,1},{1,2},{2,3},{3,0},{4,5},{5,6},{6,7},{7,4},{8,9},{9,10},{10,1... | collective-permute-start | bytes 196616 | tf_op jit(solution)/shard_map/ppermute | solution.py:20
  24.9 12.4 %collective-permute-start.8 = (bf16[3,64,256]{2,1,0:T(8,128)(2,1)S(1)}, bf16[3,64,256]{2,1,0:T(8,128)(2,1)S(1)}, u32[]{:S(2)}, u32[]{:S(2)}) collective-permute-start(bf16[3,64,256]{2,1,0:T(8,128)(2,1)S(1)} %pad_maximum_fusion.1), channel_id=1, source_target_pairs={{4,0},{8,4},{12,8},{16,12},{20,16},{24,20},{28,24},{5,1},{9,5},{13... | collective-permute-start | bytes 294920 | tf_op jit(solution)/shard_map/ppermute | solution.py:15
  26.9 9.5 %collective-permute-start.4 = (bf16[384,256]{1,0:T(8,128)(2,1)S(1)}, bf16[384,256]{1,0:T(8,128)(2,1)S(1)}, u32[]{:S(2)}, u32[]{:S(2)}) collective-permute-start(bf16[384,256]{1,0:T(8,128)(2,1)S(1)} %collective-permute-done.3.refs_6_), channel_id=1, source_target_pairs={{0,1},{1,2},{2,3},{3,0},{4,5},{5,6},{6,7},{7,4},{8,9},{9,10},{10,1... | collective-permute-start | bytes 589832 | tf_op jit(solution)/shard_map/ppermute | solution.py:20
  29.9 6.6 %collective-permute-start.9 = (bf16[64,256]{1,0:T(8,128)(2,1)S(1)}, bf16[64,256]{1,0:T(8,128)(2,1)S(1)}, u32[]{:S(2)}, u32[]{:S(2)}) collective-permute-start(bf16[64,256]{1,0:T(8,128)(2,1)S(1)} %get-tuple-element.19), channel_id=1, source_target_pairs={{4,0},{8,4},{12,8},{16,12},{20,16},{24,20},{28,24},{5,1},{9,5},{13... | collective-permute-start | bytes 98312 | tf_op jit(solution)/shard_map/ppermute | solution.py:15
  31.9 5.5 %collective-permute-start.7 = (bf16[64,256]{1,0:T(8,128)(2,1)S(1)}, bf16[64,256]{1,0:T(8,128)(2,1)S(1)}, u32[]{:S(2)}, u32[]{:S(2)}) collective-permute-start(bf16[64,256]{1,0:T(8,128)(2,1)S(1)} %get-tuple-element.20), channel_id=1, source_target_pairs={{0,4},{4,8},{8,12},{12,16},{16,20},{20,24},{24,28},{1,5},{5,9},{9,... | collective-permute-start | bytes 98312 | tf_op jit(solution)/shard_map/ppermute | solution.py:15
  36.4 8.7 %collective-permute-start.5 = (bf16[384,256]{1,0:T(8,128)(2,1)S(1)}, bf16[384,256]{1,0:T(8,128)(2,1)S(1)}, u32[]{:S(2)}, u32[]{:S(2)}) collective-permute-start(bf16[384,256]{1,0:T(8,128)(2,1)S(1)} %collective-permute-done.4.refs_7_), channel_id=1, source_target_pairs={{0,1},{1,2},{2,3},{3,0},{4,5},{5,6},{6,7},{7,4},{8,9},{9,10},{10,1... | collective-permute-start | bytes 589832 | tf_op jit(solution)/shard_map/ppermute | solution.py:20
  45.1 0.7 copy-start
  54.2 5.0 %collective-permute-start.13 = (bf16[128,256]{1,0:T(8,128)(2,1)S(1)}, bf16[128,256]{1,0:T(8,128)(2,1)S(1)}, u32[]{:S(2)}, u32[]{:S(2)}) collective-permute-start(bf16[128,256]{1,0:T(8,128)(2,1)S(1)} %pad_maximum_fusion.5.refs_1_), channel_id=1, source_target_pairs={{0,1},{1,2},{2,3},{3,0},{4,5},{5,6},{6,7},{7,4},{8,9},{9,10},{10,1... | collective-permute-start | bytes 196616 | tf_op jit(solution)/shard_map/ppermute | solution.py:20
  54.3 10.8 %collective-permute-start.16 = (bf16[384,256]{1,0:T(8,128)(2,1)S(1)}, bf16[384,256]{1,0:T(8,128)(2,1)S(1)}, u32[]{:S(2)}, u32[]{:S(2)}) collective-permute-start(bf16[384,256]{1,0:T(8,128)(2,1)S(1)} %slice.92.refs_5_), channel_id=1, source_target_pairs={{0,1},{1,2},{2,3},{3,0},{4,5},{5,6},{6,7},{7,4},{8,9},{9,10},{10,1... | collective-permute-start | bytes 589832 | tf_op jit(solution)/shard_map/ppermute | solution.py:20
  59.2 5.9 %collective-permute-start.14 = (bf16[128,256]{1,0:T(8,128)(2,1)S(1)}, bf16[128,256]{1,0:T(8,128)(2,1)S(1)}, u32[]{:S(2)}, u32[]{:S(2)}) collective-permute-start(bf16[128,256]{1,0:T(8,128)(2,1)S(1)} %collective-permute-done.13.refs_2_), channel_id=1, source_target_pairs={{0,1},{1,2},{2,3},{3,0},{4,5},{5,6},{6,7},{7,4},{8,9},{9,10},{10,1... | collective-permute-start | bytes 196616 | tf_op jit(solution)/shard_map/ppermute | solution.py:20
  65.1 6.7 %collective-permute-start.17 = (bf16[384,256]{1,0:T(8,128)(2,1)S(1)}, bf16[384,256]{1,0:T(8,128)(2,1)S(1)}, u32[]{:S(2)}, u32[]{:S(2)}) collective-permute-start(bf16[384,256]{1,0:T(8,128)(2,1)S(1)} %collective-permute-done.16.refs_6_), channel_id=1, source_target_pairs={{0,1},{1,2},{2,3},{3,0},{4,5},{5,6},{6,7},{7,4},{8,9},{9,10},{10,1... | collective-permute-start | bytes 589832 | tf_op jit(solution)/shard_map/ppermute | solution.py:20
  65.2 18.3 %collective-permute-start.19 = (bf16[3,64,256]{2,1,0:T(8,128)(2,1)S(1)}, bf16[3,64,256]{2,1,0:T(8,128)(2,1)S(1)}, u32[]{:S(2)}, u32[]{:S(2)}) collective-permute-start(bf16[3,64,256]{2,1,0:T(8,128)(2,1)S(1)} %pad_maximum_fusion.2), channel_id=1, source_target_pairs={{0,4},{4,8},{8,12},{12,16},{16,20},{20,24},{24,28},{1,5},{5,9},{9,... | collective-permute-start | bytes 294920 | tf_op jit(solution)/shard_map/ppermute | solution.py:15
  69.8 6.2 %collective-permute-start.15 = (bf16[128,256]{1,0:T(8,128)(2,1)S(1)}, bf16[128,256]{1,0:T(8,128)(2,1)S(1)}, u32[]{:S(2)}, u32[]{:S(2)}) collective-permute-start(bf16[128,256]{1,0:T(8,128)(2,1)S(1)} %collective-permute-done.14.refs_3_), channel_id=1, source_target_pairs={{0,1},{1,2},{2,3},{3,0},{4,5},{5,6},{6,7},{7,4},{8,9},{9,10},{10,1... | collective-permute-start | bytes 196616 | tf_op jit(solution)/shard_map/ppermute | solution.py:20
  69.9 13.6 %collective-permute-start.21 = (bf16[3,64,256]{2,1,0:T(8,128)(2,1)S(1)}, bf16[3,64,256]{2,1,0:T(8,128)(2,1)S(1)}, u32[]{:S(2)}, u32[]{:S(2)}) collective-permute-start(bf16[3,64,256]{2,1,0:T(8,128)(2,1)S(1)} %pad_maximum_fusion.3), channel_id=1, source_target_pairs={{4,0},{8,4},{12,8},{16,12},{20,16},{24,20},{28,24},{5,1},{9,5},{13... | collective-permute-start | bytes 294920 | tf_op jit(solution)/shard_map/ppermute | solution.py:15
  71.8 11.7 %collective-permute-start.18 = (bf16[384,256]{1,0:T(8,128)(2,1)S(1)}, bf16[384,256]{1,0:T(8,128)(2,1)S(1)}, u32[]{:S(2)}, u32[]{:S(2)}) collective-permute-start(bf16[384,256]{1,0:T(8,128)(2,1)S(1)} %collective-permute-done.17.refs_7_), channel_id=1, source_target_pairs={{0,1},{1,2},{2,3},{3,0},{4,5},{5,6},{6,7},{7,4},{8,9},{9,10},{10,1... | collective-permute-start | bytes 589832 | tf_op jit(solution)/shard_map/ppermute | solution.py:20
  76.0 6.5 %collective-permute-start.22 = (bf16[64,256]{1,0:T(8,128)(2,1)S(1)}, bf16[64,256]{1,0:T(8,128)(2,1)S(1)}, u32[]{:S(2)}, u32[]{:S(2)}) collective-permute-start(bf16[64,256]{1,0:T(8,128)(2,1)S(1)} %get-tuple-element.13), channel_id=1, source_target_pairs={{4,0},{8,4},{12,8},{16,12},{20,16},{24,20},{28,24},{5,1},{9,5},{13... | collective-permute-start | bytes 98312 | tf_op jit(solution)/shard_map/ppermute | solution.py:15
  78.4 5.1 %collective-permute-start.20 = (bf16[64,256]{1,0:T(8,128)(2,1)S(1)}, bf16[64,256]{1,0:T(8,128)(2,1)S(1)}, u32[]{:S(2)}, u32[]{:S(2)}) collective-permute-start(bf16[64,256]{1,0:T(8,128)(2,1)S(1)} %get-tuple-element.14), channel_id=1, source_target_pairs={{0,4},{4,8},{8,12},{12,16},{16,20},{20,24},{24,28},{1,5},{5,9},{9,... | collective-permute-start | bytes 98312 | tf_op jit(solution)/shard_map/ppermute | solution.py:15

commit v2 on v0

v2 whole, which is shorter than its diff:
```python
import jax
import jax.numpy as jnp
from jax import lax
from jax.experimental import pallas as pl
from jax.experimental.pallas import tpu as pltpu
from jax.sharding import PartitionSpec as P

WIDTH = 64
LANES = 128


def shift_along(block, axis, step):
    count = lax.axis_size(axis)
    pairs = [(i, i + step) for i in range(count) if 0 <= i + step < count]
    return lax.ppermute(block, axis, pairs)


def ring(block, axis, step=1):
    count = lax.axis_size(axis)
    return lax.ppermute(block, axis, [(i, (i + step) % count) for i in range(count)])


def column_of(row, lanes=LANES):
    return jnp.broadcast_to(row, (lanes, row.shape[1])).T[:, :1]


def row_of(column, lanes=LANES):
    return jnp.broadcast_to(column, (column.shape[0], lanes)).T[:1]


def silu(values):
    return values / (1.0 + jnp.exp(-values))


def inverse_rms(row, total):
    return 1.0 / jnp.sqrt(column_of(row) / total + 1e-6)


def conv_kernel(pieces, normed, last, total, *refs):
    place, refs = refs[0], refs[1:]
    cells_in, refs = refs[:pieces], refs[pieces:]
    if not normed:
        (gain, sums), refs = refs[:2], refs[2:]
    (taps, start), refs = refs[:2], refs[2:]
    if last == "out":
        source, refs = refs[0], refs[1:]
    outs, acts = refs[:-1], refs[-1]
    if pieces == 3:
        joined = [ref[...] for ref in cells_in]
    else:
        top, edge, body, low = cells_in
        joined = [top[...], edge[:WIDTH], body[...], edge[WIDTH:], low[...]]
    values = jnp.concatenate(joined, axis=0).astype(jnp.float32)
    if not normed:
        values = silu(values * gain[...] * inverse_rms(sums[...], total))
    length, width = values.shape
    cells = length - 2 * WIDTH
    column = lax.broadcasted_iota(jnp.int32, (length, 1), 0) % WIDTH
    acts[1] = values.astype(jnp.bfloat16)
    before = jnp.where(column == 0, 0.0, pltpu.roll(values, 1, 0))
    acts[0] = before.astype(jnp.bfloat16)
    after = jnp.where(column == WIDTH - 1, 0.0, pltpu.roll(values, length - 1, 0))
    acts[2] = after.astype(jnp.bfloat16)
    lanes = pl.ds(pl.multiple_of(place[0] * width, width), width)
    left = [acts[s, q * WIDTH : q * WIDTH + cells] for q in range(3) for s in range(3)]
    right = [taps[t, :, lanes] for t in range(9)]
    result = start[...] + lax.dot_general(
        jnp.concatenate(left, axis=1),
        jnp.concatenate(right, axis=1),
        (((1,), (1,)), ((), ())),
        preferred_element_type=jnp.float32,
    )
    if last == "out":
        outs[0][...] = (result + source[...].astype(jnp.float32)).T.astype(outs[0].dtype)
    else:
        outs[0][...] = result
    if last == "sums":
        outs[1][...] = row_of(jnp.sum(result * result, axis=1, keepdims=True))


VMEM = pl.BlockSpec(memory_space=pltpu.VMEM)
PARAMS = pltpu.CompilerParams(vmem_limit_bytes=16 << 20)


def conv_part(owner, cells_in, norm, taps, start, total, last="", source=None):
    outs, width = taps.shape[1], cells_in[0].shape[1]
    length = sum(piece.shape[0] for piece in cells_in)
    cells = length - 2 * WIDTH
    operands = [owner, *cells_in, *norm, taps, start]
    if source is not None:
        operands.append(source)
    shapes = [jax.ShapeDtypeStruct((cells, outs), jnp.float32)]
    if last == "out":
        shapes = [jax.ShapeDtypeStruct((outs, cells), jnp.bfloat16)]
    if last == "sums":
        shapes.append(jax.ShapeDtypeStruct((1, cells), jnp.float32))
    pieces, first = len(cells_in), start.shape[0] == 1

    def kernel(*refs):
        conv_kernel(pieces, not norm, last, total, *refs)

    alias = {} if first or last == "out" else {len(operands) - 1: 0}
    result = pl.pallas_call(
        kernel,
        out_shape=shapes,
        in_specs=[pl.BlockSpec(memory_space=pltpu.SMEM)] + [VMEM] * (len(operands) - 1),
        out_specs=[VMEM] * len(shapes),
        input_output_aliases=alias,
        scratch_shapes=[pltpu.VMEM((3, length, width), jnp.bfloat16)],
        compiler_params=PARAMS,
    )(*operands)
    return result if len(result) > 1 else result[0]


def fetch_kernel(frame, weights, taps, sems):
    copies = [
        pltpu.make_async_copy(weights.at[frame, q, s], taps.at[q * 3 + s], sems.at[q * 3 + s])
        for q in range(3)
        for s in range(3)
    ]
    for copy in copies:
        copy.start()
    for copy in copies:
        copy.wait()


def fetch(weights):
    outs, total = weights.shape[3:]
    return pl.pallas_call(
        lambda *refs: fetch_kernel(weights.shape[0] - 1, *refs),
        out_shape=pltpu.VMEM((9, outs, total), weights.dtype),
        in_specs=[pl.BlockSpec(memory_space=pltpu.HBM)],
        out_specs=VMEM,
        scratch_shapes=[pltpu.SemaphoreType.DMA((9,))],
        compiler_params=PARAMS,
    )(pltpu.with_memory_space_constraint(weights, pltpu.HBM))


def act_kernel(total, values, gain, sums, out):
    out[...] = silu(values[...] * gain[...] * inverse_rms(sums[...], total)).astype(out.dtype)


def act(values, gain, sums, total):
    return pl.pallas_call(
        lambda *refs: act_kernel(total, *refs),
        out_shape=jax.ShapeDtypeStruct(values.shape, jnp.bfloat16),
        in_specs=[VMEM] * 3,
        out_specs=VMEM,
        compiler_params=PARAMS,
    )(values, gain, sums)


def edges_of(block):
    return block[:WIDTH], block[block.shape[0] - WIDTH :]


def halo(top, low):
    count = lax.axis_size("rows")
    even = lax.axis_index("rows") % 2 == 0
    rounds = []
    for begin in range(2):
        pairs = [(i, i + 1) for i in range(begin, count - 1, 2)]
        send = jnp.where(even, low, top) if begin == 0 else jnp.where(even, top, low)
        rounds.append(lax.ppermute(send, "rows", pairs + [(b, a) for a, b in pairs]))
    return jnp.where(even, rounds[1], rounds[0]), jnp.where(even, rounds[0], rounds[1])


def others(value, axis):
    return [ring(value, axis, step) for step in range(1, lax.axis_size(axis))]


def conv_stage(block, groups, norms, weights, bias, total, last, source=None, halos=()):
    count = lax.axis_size("chan")
    place = lax.axis_index("chan").astype(jnp.int32)
    cells = block.shape[0]
    result = bias.reshape(1, -1)
    taps = fetch(weights)
    blocks = [block]
    for _ in range(1, count - 1):
        blocks.append(ring(blocks[-1], "chan"))
    edges = [edges_of(b) for b in blocks]
    edge = ring(jnp.concatenate(edges[-1], axis=0), "chan")
    edges.append((edge[:WIDTH], edge[WIDTH:]))
    body = ring(blocks[-1][WIDTH : cells - WIDTH], "chan")
    halos = list(halos)
    for group in groups:
        pair = halo(*[jnp.stack([edges[r][side] for r in group]) for side in range(2)])
        halos += [(pair[0][k], pair[1][k]) for k in range(len(group))]
    for r in range(count):
        up, down = halos[r]
        end = r == count - 1
        pieces = [up, edge, body, down] if end else [up, blocks[r], down]
        owner = lax.rem(place + count - r, count).reshape(1)
        result = conv_part(
            owner, pieces, norms[r], taps, result, total, last if end else "", source if end else None
        )
    return result


def groups_of(count):
    return [range(1, count)], [range(count - 2), range(count - 2, count)]


def padded(block, width):
    low = shift_along(block[..., block.shape[-1] - width :], "rows", 1)
    high = shift_along(block[..., :width], "rows", -1)
    return jnp.concatenate([low, block, high], axis=-1)


def activate(values, gain, total):
    mean_sq = lax.psum(jnp.sum(values * values, axis=0, keepdims=True), "chan") / total
    return jax.nn.silu(values * gain[:, None, None] / jnp.sqrt(mean_sq + 1e-06)).astype(jnp.bfloat16)


def convolve(block, kernel):
    whole = padded(lax.all_gather(block, "chan", axis=0, tiled=True), WIDTH)
    channels, frames, cells = whole.shape
    grid = whole.reshape(1, channels, frames, cells // WIDTH, WIDTH)
    result = lax.conv_general_dilated(
        grid,
        kernel,
        (1, 1, 1),
        ((2, 0), (0, 0), (1, 1)),
        dimension_numbers=("NCDHW", "DHWOI", "NCDHW"),
        preferred_element_type=jnp.float32,
    )
    return result[0].reshape(kernel.shape[3], frames, cells - 2 * WIDTH)


def general(features, gain_first, weight_first, bias_first, gain_second, weight_second, bias_second):
    total = weight_first.shape[4]
    source = features.astype(jnp.float32)
    middle = convolve(activate(source, gain_first, total), weight_first) + bias_first[:, None, None]
    result = convolve(activate(middle, gain_second, total), weight_second)
    return (source + result + bias_second[:, None, None]).astype(jnp.bfloat16)


def on_device(
    features, gain_first, weight_first, bias_first, gain_second, weight_second, bias_second
):
    channels, frames, cells = features.shape
    count = lax.axis_size("chan")
    if frames != 1 or channels % LANES or cells < 3 * WIDTH or count < 3:
        return general(
            features, gain_first, weight_first, bias_first, gain_second, weight_second, bias_second
        )
    out = resident(
        features, gain_first, weight_first, bias_first, gain_second, weight_second, bias_second
    )
    return out


def resident(
    features, gain_first, weight_first, bias_first, gain_second, weight_second, bias_second
):
    channels, frames, cells = features.shape
    count, total = lax.axis_size("chan"), weight_first.shape[4]
    first, then = groups_of(count)
    block = features.reshape(channels, cells).T
    own_halo = halo(*edges_of(block))
    source = jnp.concatenate([own_halo[0], block, own_halo[1]], axis=0).astype(jnp.float32)
    sums = jnp.sum(source * source, axis=1)
    note = jnp.concatenate([sums, gain_first])
    notes = [note] + others(note, "chan")
    length = sums.shape[0]
    sums = sum(note[:length] for note in notes).reshape(1, -1)
    norms = [(note[length:].reshape(1, -1), sums) for note in notes]
    middle, sums = conv_stage(
        block, first, norms, weight_first, bias_first, total, "sums", halos=[own_halo]
    )
    sums = sums + sum(others(sums, "chan"))
    second = act(middle, gain_second.reshape(1, -1), sums, total)
    out = conv_stage(second, then, [()] * count, weight_second, bias_second, total, "out", block)
    return out.reshape(channels, frames, cells)


def solution(mesh):
    in_specs = (
        P("chan", None, "rows"),
        P("chan"),
        P(None, None, None, "chan", None),
        P("chan"),
        P("chan"),
        P(None, None, None, "chan", None),
        P("chan"),
    )
    return jax.shard_map(
        on_device, mesh=mesh, in_specs=in_specs, out_specs=P("chan", None, "rows"), check_vma=False
    )
```

time: 155 us -> 95.4 us (0.62)
  the two profiles are of different devices: /device:TPU:3 before, /device:TPU:0 now
where the time goes in v2:
time: 95.4 us; the launch traced here: 95.2 us
  waiting for transfers between devices  46.3 us (49%)
  starting transfers between devices  28.4 us (30%)
  Pallas kernels  14 us (15%)
  local copies, waits for them, and re-layouts  5.74 us (6%)
    ppermute x14, waiting for transfers between devices, ring(): lax.ppermute(block, axis, [(i, (i + step) % count) for i in range(count)])  46.3 us
    ppermute x14, starting transfers between devices, ring(): lax.ppermute(block, axis, [(i, (i + step) % count) for i in range(count)])  14.9 us
    ppermute x8, starting transfers between devices, halo(): lax.ppermute(send, 'rows', pairs + [(b, a) for a, b in pairs])  13.5 us
    pallas_call x8, Pallas kernels, conv_part(): pl.pallas_call(kernel, out_shape=shapes, in_specs=[pl.BlockSpec(memory_sp...  8.93 us
    unnamed x13, local copies, waits for them, and re-layouts  5.6 us
    pallas_call x2, Pallas kernels, fetch(): pl.pallas_call(lambda *refs: fetch_kernel(weights.shape[0] - 1, *refs), o...  4.76 us
  transfers between devices with their start and end apart: 22, of which 10 were waited for; matrix products, arithmetic and copies ran while one was open for 0% of the time, Pallas kernels for 11%

profile of v2, /device:TPU:0, one launch (start us, length us, event | category | flops | bytes accessed | tf_op | source)
XLA Modules:
  0.0 95.2 jit_solution(16446773353142535591)
XLA Ops:
  0.0 1.1 %copy.13 = bf16[256,1,512]{0,2,1:T(8,128)(2,1)S(1)} copy(bf16[256,1,512]{2,0,1:T(8,128)(2,1)} %param.7) | data formatting | bytes 524288 | tf_op args[0]
  1.1 3.1 %collective-permute-start = (bf16[512,256]{1,0:T(8,128)(2,1)S(1)}, bf16[512,256]{1,0:T(8,128)(2,1)S(1)}, u32[]{:S(2)}, u32[]{:S(2)}) collective-permute-start(bf16[512,256]{1,0:T(8,128)(2,1)S(1)} %bitcast.71), channel_id=1, source_target_pairs={{0,1},{1,2},{2,3},{3,0},{4,5},{5,6},{6,7},{7,4},{8,9},{9,10},{10,1... | collective-permute-start | bytes 786440 | tf_op jit(solution)/shard_map/ppermute | solution.py:20
  4.2 0.7 collective-permute-start.6
  4.9 2.9 %collective-permute-start.7 = (bf16[64,256]{1,0:T(8,128)(2,1)S(1)}, bf16[64,256]{1,0:T(8,128)(2,1)S(1)}, u32[]{:S(2)}, u32[]{:S(2)}) collective-permute-start(bf16[64,256]{1,0:T(8,128)(2,1)S(1)} %get-tuple-element.18), channel_id=1, source_target_pairs={{0,4},{8,12},{16,20},{24,28},{4,0},{12,8},{20,16},{28,24},{1,5},{9... | collective-permute-start | bytes 98312 | tf_op jit(solution)/shard_map/ppermute | solution.py:164
  7.8 2.4 %shard_map.73.refs_6_.refs_7_ = bf16[9,256,1024]{2,1,0:T(8,128)(2,1)S(1)} custom-call(bf16[3,3,3,256,1024]{4,3,2,1,0:T(8,128)(2,1)} %refs_0_.2), custom_call_target="tpu_custom_call" | custom-call | tf_op jit(solution)/shard_map/pallas_call | solution.py:129
  10.2 2.1 %copy-done = bf16[9,256,1024]{2,1,0:T(8,128)(2,1)} copy-done((bf16[9,256,1024]{2,1,0:T(8,128)(2,1)}, bf16[9,256,1024]{2,1,0:T(8,128)(2,1)S(1)}, u32[]{:S(2)}) %copy-start) | copy-done | bytes 4718616
  12.4 0.2 collective-permute-done.refs_2_
  12.6 1.4 %collective-permute-start.1 = (bf16[512,256]{1,0:T(8,128)(2,1)S(1)}, bf16[512,256]{1,0:T(8,128)(2,1)S(1)}, u32[]{:S(2)}, u32[]{:S(2)}) collective-permute-start(bf16[512,256]{1,0:T(8,128)(2,1)S(1)} %collective-permute-done.refs_2_), channel_id=1, source_target_pairs={{0,1},{1,2},{2,3},{3,0},{4,5},{5,6},{6,7},{7,4},{8,9},{9,10},{10,1... | collective-permute-start | bytes 786440 | tf_op jit(solution)/shard_map/ppermute | solution.py:20
  14.0 0.0 collective-permute-done.6
  14.0 0.2 multiply_reduce_fusion
  14.2 1.3 %collective-permute-start.10 = (f32[896]{0:T(1024)S(1)}, f32[896]{0:T(1024)S(1)}, u32[]{:S(2)}, u32[]{:S(2)}) collective-permute-start(f32[896]{0:T(1024)S(1)} %pad_maximum_fusion.8), channel_id=1, source_target_pairs={{0,2},{1,3},{2,0},{3,1},{4,6},{5,7},{6,4},{7,5},{8,10},{9,11},{10,... | collective-permute-start | bytes 10760 | tf_op jit(solution)/shard_map/ppermute | solution.py:20
  15.5 2.7 %collective-permute-start.8 = (f32[896]{0:T(1024)S(1)}, f32[896]{0:T(1024)S(1)}, u32[]{:S(2)}, u32[]{:S(2)}) collective-permute-start(f32[896]{0:T(1024)S(1)} %pad_maximum_fusion.8), channel_id=1, source_target_pairs={{0,3},{1,0},{2,1},{3,2},{4,7},{5,4},{6,5},{7,6},{8,11},{9,8},{10,9... | collective-permute-start | bytes 10760 | tf_op jit(solution)/shard_map/ppermute | solution.py:20
  18.2 4.4 %collective-permute-done.1.refs_2_ = bf16[512,256]{1,0:T(8,128)(2,1)S(1)} collective-permute-done((bf16[512,256]{1,0:T(8,128)(2,1)S(1)}, bf16[512,256]{1,0:T(8,128)(2,1)S(1)}, u32[]{:S(2)}, u32[]{:S(2)}) %collective-permute-start.1) | collective-permute-done | bytes 262176 | tf_op jit(solution)/shard_map/ppermute | solution.py:20
  22.6 0.1 collective-permute-start.2
  22.7 6.0 %collective-permute-done.2.refs_2_ = bf16[128,256]{1,0:T(8,128)(2,1)S(1)} collective-permute-done((bf16[128,256]{1,0:T(8,128)(2,1)S(1)}, bf16[128,256]{1,0:T(8,128)(2,1)S(1)}, u32[]{:S(2)}, u32[]{:S(2)}) %collective-permute-start.2) | collective-permute-done | bytes 65568 | tf_op jit(solution)/shard_map/ppermute | solution.py:20
  28.8 0.7 collective-permute-start.3
  29.5 2.9 %collective-permute-start.4 = (bf16[3,64,256]{2,1,0:T(8,128)(2,1)S(1)}, bf16[3,64,256]{2,1,0:T(8,128)(2,1)S(1)}, u32[]{:S(2)}, u32[]{:S(2)}) collective-permute-start(bf16[3,64,256]{2,1,0:T(8,128)(2,1)S(1)} %get-tuple-element.27), channel_id=1, source_target_pairs={{0,4},{8,12},{16,20},{24,28},{4,0},{12,8},{20,16},{28,24},{1,5},{9... | collective-permute-start | bytes 294920 | tf_op jit(solution)/shard_map/ppermute | solution.py:164
  32.4 2.3 %copy-done.1 = bf16[9,256,1024]{2,1,0:T(8,128)(2,1)S(1)} copy-done((bf16[9,256,1024]{2,1,0:T(8,128)(2,1)S(1)}, bf16[9,256,1024]{2,1,0:T(8,128)(2,1)}, u32[]{:S(2)}) %copy-start.1) | copy-done | bytes 4718616
  34.8 1.1 %shard_map.74.refs_7_ = f32[512,256]{1,0:T(8,128)S(1)} custom-call(s32[1]{0:T(128)} %bitcast.21.refs_0_, bf16[64,256]{1,0:T(8,128)(2,1)S(1)} %get-tuple-element.53.refs_1_, bf16[512,256]{1,0:T(8,128)(2,1)S(1)} %bitcast.74, bf16[64,256]{1,0:T(8,128)(2,1)S(1)} %get-tuple-element.54.refs_3_, f32[1,256]{1,0:T(1,128)S(1)} %bitcast.77, ...), custom_call_target="tpu_custom_call" | custom-call | tf_op jit(solution)/shard_map/pallas_call | solution.py:103
  36.0 0.1 collective-permute-start.5
  36.1 1.2 %shard_map.75.refs_7_ = f32[512,256]{1,0:T(8,128)S(1)} custom-call(s32[1]{0:T(128)} %bitcast.17.refs_0_, bf16[64,256]{1,0:T(8,128)(2,1)S(1)} %get-tuple-element.59.refs_1_, bf16[512,256]{1,0:T(8,128)(2,1)S(1)} %collective-permute-done.refs_2_, bf16[64,256]{1,0:T(8,128)(2,1)S(1)} %get-tuple-element.37.refs_3_, ...), custom_call_target="tpu_custom_call", output_to_operand_aliasing={{}: (7, {})} | custom-call | tf_op jit(solution)/shard_map/pallas_call | solution.py:103
  37.3 1.2 %shard_map.76.refs_8_ = f32[512,256]{1,0:T(8,128)S(1)} custom-call(s32[1]{0:T(128)} %bitcast.13.refs_0_, bf16[64,256]{1,0:T(8,128)(2,1)S(1)} %get-tuple-element.58.refs_1_, bf16[512,256]{1,0:T(8,128)(2,1)S(1)} %collective-permute-done.1.refs_2_, bf16[64,256]{1,0:T(8,128)(2,1)S(1)} %get-tuple-element.38.refs_3_, ...), custom_call_target="tpu_custom_call", output_to_operand_aliasing={{}: (7, {})} | custom-call | tf_op jit(solution)/shard_map/pallas_call | solution.py:103
  38.4 0.0 copy-start.4
  38.5 6.2 %collective-permute-done.5.refs_3_ = bf16[384,256]{1,0:T(8,128)(2,1)S(1)} collective-permute-done((bf16[384,256]{1,0:T(8,128)(2,1)S(1)}, bf16[384,256]{1,0:T(8,128)(2,1)S(1)}, u32[]{:S(2)}, u32[]{:S(2)}) %collective-permute-start.5) | collective-permute-done | bytes 196640 | tf_op jit(solution)/shard_map/ppermute | solution.py:20
  44.7 1.3 %shard_map.77 = (f32[512,256]{1,0:T(8,128)S(1)}, f32[1,512]{1,0:T(1,128)S(1)}) custom-call(s32[1]{0:T(128)} %bitcast.refs_0_, bf16[64,256]{1,0:T(8,128)(2,1)S(1)} %get-tuple-element.57.refs_1_, bf16[128,256]{1,0:T(8,128)(2,1)S(1)} %collective-permute-done.2.refs_2_, ...), custom_call_target="tpu_custom_call", output_to_operand_aliasing={{0}: (8, {})} | custom-call | tf_op jit(solution)/shard_map/pallas_call | solution.py:103
  46.0 0.0 collective-permute-start.11
  46.0 0.1 collective-permute-start.12
  46.1 3.7 %collective-permute-start.13 = (f32[1,512]{1,0:T(1,128)S(1)}, f32[1,512]{1,0:T(1,128)S(1)}, u32[]{:S(2)}, u32[]{:S(2)}) collective-permute-start(f32[1,512]{1,0:T(1,128)S(1)} %get-tuple-element.8), channel_id=1, source_target_pairs={{0,3},{1,0},{2,1},{3,2},{4,7},{5,4},{6,5},{7,6},{8,11},{9,8},{10,9... | collective-permute-start | bytes 6152 | tf_op jit(solution)/shard_map/ppermute | solution.py:20
  49.8 1.6 %collective-permute-done.11 = f32[1,512]{1,0:T(1,128)S(1)} collective-permute-done((f32[1,512]{1,0:T(1,128)S(1)}, f32[1,512]{1,0:T(1,128)S(1)}, u32[]{:S(2)}, u32[]{:S(2)}) %collective-permute-start.11) | collective-permute-done | bytes 2080 | tf_op jit(solution)/shard_map/ppermute | solution.py:20
  51.4 0.6 collective-permute-done.13
  52.0 0.3 shard_map.78.refs_2_
  52.3 2.1 %collective-permute-start.14 = (bf16[512,256]{1,0:T(8,128)(2,1)S(1)}, bf16[512,256]{1,0:T(8,128)(2,1)S(1)}, u32[]{:S(2)}, u32[]{:S(2)}) collective-permute-start(bf16[512,256]{1,0:T(8,128)(2,1)S(1)} %shard_map.78.refs_2_), channel_id=1, source_target_pairs={{0,1},{1,2},{2,3},{3,0},{4,5},{5,6},{6,7},{7,4},{8,9},{9,10},{10,1... | collective-permute-start | bytes 786440 | tf_op jit(solution)/shard_map/ppermute | solution.py:20
  54.4 6.1 %collective-permute-done.14.refs_2_ = bf16[512,256]{1,0:T(8,128)(2,1)S(1)} collective-permute-done((bf16[512,256]{1,0:T(8,128)(2,1)S(1)}, bf16[512,256]{1,0:T(8,128)(2,1)S(1)}, u32[]{:S(2)}, u32[]{:S(2)}) %collective-permute-start.14) | collective-permute-done | bytes 262176 | tf_op jit(solution)/shard_map/ppermute | solution.py:20
  60.5 0.7 collective-permute-start.20
  61.2 2.9 %collective-permute-start.21 = (bf16[2,64,256]{2,1,0:T(8,128)(2,1)S(1)}, bf16[2,64,256]{2,1,0:T(8,128)(2,1)S(1)}, u32[]{:S(2)}, u32[]{:S(2)}) collective-permute-start(bf16[2,64,256]{2,1,0:T(8,128)(2,1)S(1)} %get-tuple-element.31), channel_id=1, source_target_pairs={{0,4},{8,12},{16,20},{24,28},{4,0},{12,8},{20,16},{28,24},{1,5},{9... | collective-permute-start | bytes 196616 | tf_op jit(solution)/shard_map/ppermute | solution.py:164
  64.1 0.2 collective-permute-start.15
  64.4 2.4 %shard_map.79.refs_4_.refs_5_ = bf16[9,256,1024]{2,1,0:T(8,128)(2,1)S(1)} custom-call(bf16[3,3,3,256,1024]{4,3,2,1,0:T(8,128)(2,1)} %refs_0_.3), custom_call_target="tpu_custom_call" | custom-call | tf_op jit(solution)/shard_map/pallas_call | solution.py:129
  66.8 7.4 %collective-permute-done.15.refs_2_ = bf16[512,256]{1,0:T(8,128)(2,1)S(1)} collective-permute-done((bf16[512,256]{1,0:T(8,128)(2,1)S(1)}, bf16[512,256]{1,0:T(8,128)(2,1)S(1)}, u32[]{:S(2)}, u32[]{:S(2)}) %collective-permute-start.15) | collective-permute-done | bytes 262176 | tf_op jit(solution)/shard_map/ppermute | solution.py:20
  74.2 0.1 collective-permute-start.16
  74.3 6.0 %collective-permute-done.16.refs_2_ = bf16[128,256]{1,0:T(8,128)(2,1)S(1)} collective-permute-done((bf16[128,256]{1,0:T(8,128)(2,1)S(1)}, bf16[128,256]{1,0:T(8,128)(2,1)S(1)}, u32[]{:S(2)}, u32[]{:S(2)}) %collective-permute-start.16) | collective-permute-done | bytes 65568 | tf_op jit(solution)/shard_map/ppermute | solution.py:20
  80.4 0.7 collective-permute-start.17
  81.1 2.1 %collective-permute-start.18 = (bf16[2,64,256]{2,1,0:T(8,128)(2,1)S(1)}, bf16[2,64,256]{2,1,0:T(8,128)(2,1)S(1)}, u32[]{:S(2)}, u32[]{:S(2)}) collective-permute-start(bf16[2,64,256]{2,1,0:T(8,128)(2,1)S(1)} %get-tuple-element.35), channel_id=1, source_target_pairs={{0,4},{8,12},{16,20},{24,28},{4,0},{12,8},{20,16},{28,24},{1,5},{9... | collective-permute-start | bytes 196616 | tf_op jit(solution)/shard_map/ppermute | solution.py:164
  83.2 0.8 shard_map.80.refs_5_
  84.0 0.8 shard_map.81.refs_5_
  84.9 0.1 collective-permute-start.19
  85.0 0.8 shard_map.82.refs_6_
  85.9 7.7 %collective-permute-done.19.refs_3_ = bf16[384,256]{1,0:T(8,128)(2,1)S(1)} collective-permute-done((bf16[384,256]{1,0:T(8,128)(2,1)S(1)}, bf16[384,256]{1,0:T(8,128)(2,1)S(1)}, u32[]{:S(2)}, u32[]{:S(2)}) %collective-permute-start.19) | collective-permute-done | bytes 196640 | tf_op jit(solution)/shard_map/ppermute | solution.py:20
  93.6 1.6 %shard_map.83 = bf16[256,512]{1,0:T(8,128)(2,1)} custom-call(s32[1]{0:T(128)} %bitcast.refs_0_, bf16[64,256]{1,0:T(8,128)(2,1)S(1)} %get-tuple-element.50.refs_1_, bf16[128,256]{1,0:T(8,128)(2,1)S(1)} %collective-permute-done.16.refs_2_, bf16[384,256]{1,0:T(8,128)(2,1)S(1)} %collective-permute-done.19.refs_3_, ...), custom_call_target="tpu_custom_call" | custom-call | tf_op jit(solution)/shard_map/pallas_call | solution.py:103
  (52 shorter events, 0.3 us)
Async XLA Ops:
  0.0 14.2 %copy-start.2 = (f32[256]{0:T(256)S(1)}, f32[256]{0:T(256)}, u32[]{:S(2)}) copy-start(f32[256]{0:T(256)} %param.8) | copy-start | bytes 3076
  0.0 32.4 %copy-start.5 = (f32[256]{0:T(256)S(1)}, f32[256]{0:T(256)}, u32[]{:S(2)}) copy-start(f32[256]{0:T(256)} %param.10) | copy-start | bytes 3076
  1.1 11.4 %collective-permute-start = (bf16[512,256]{1,0:T(8,128)(2,1)S(1)}, bf16[512,256]{1,0:T(8,128)(2,1)S(1)}, u32[]{:S(2)}, u32[]{:S(2)}) collective-permute-start(bf16[512,256]{1,0:T(8,128)(2,1)S(1)} %bitcast.71), channel_id=1, source_target_pairs={{0,1},{1,2},{2,3},{3,0},{4,5},{5,6},{6,7},{7,4},{8,9},{9,10},{10,1... | collective-permute-start | bytes 786440 | tf_op jit(solution)/shard_map/ppermute | solution.py:20
  4.2 9.7 %collective-permute-start.6 = (bf16[64,256]{1,0:T(8,128)(2,1)S(1)}, bf16[64,256]{1,0:T(8,128)(2,1)S(1)}, u32[]{:S(2)}, u32[]{:S(2)}) collective-permute-start(bf16[64,256]{1,0:T(8,128)(2,1)S(1)} %get-tuple-element.17), channel_id=1, source_target_pairs={{4,8},{12,16},{20,24},{8,4},{16,12},{24,20},{5,9},{13,17},{21,25},... | collective-permute-start | bytes 98312 | tf_op jit(solution)/shard_map/ppermute | solution.py:164
  4.9 9.1 %collective-permute-start.7 = (bf16[64,256]{1,0:T(8,128)(2,1)S(1)}, bf16[64,256]{1,0:T(8,128)(2,1)S(1)}, u32[]{:S(2)}, u32[]{:S(2)}) collective-permute-start(bf16[64,256]{1,0:T(8,128)(2,1)S(1)} %get-tuple-element.18), channel_id=1, source_target_pairs={{0,4},{8,12},{16,20},{24,28},{4,0},{12,8},{20,16},{28,24},{1,5},{9... | collective-permute-start | bytes 98312 | tf_op jit(solution)/shard_map/ppermute | solution.py:164
  10.2 2.2 %copy-start = (bf16[9,256,1024]{2,1,0:T(8,128)(2,1)}, bf16[9,256,1024]{2,1,0:T(8,128)(2,1)S(1)}, u32[]{:S(2)}) copy-start(bf16[9,256,1024]{2,1,0:T(8,128)(2,1)S(1)} %shard_map.73.refs_6_.refs_7_) | copy-start | bytes 14155780
  12.4 39.6 %copy-start.3 = (f32[256]{0:T(256)S(1)}, f32[256]{0:T(256)}, u32[]{:S(2)}) copy-start(f32[256]{0:T(256)} %param.11) | copy-start | bytes 3076
  12.6 10.1 %collective-permute-start.1 = (bf16[512,256]{1,0:T(8,128)(2,1)S(1)}, bf16[512,256]{1,0:T(8,128)(2,1)S(1)}, u32[]{:S(2)}, u32[]{:S(2)}) collective-permute-start(bf16[512,256]{1,0:T(8,128)(2,1)S(1)} %collective-permute-done.refs_2_), channel_id=1, source_target_pairs={{0,1},{1,2},{2,3},{3,0},{4,5},{5,6},{6,7},{7,4},{8,9},{9,10},{10,1... | collective-permute-start | bytes 786440 | tf_op jit(solution)/shard_map/ppermute | solution.py:20
  14.2 18.2 %collective-permute-start.10 = (f32[896]{0:T(1024)S(1)}, f32[896]{0:T(1024)S(1)}, u32[]{:S(2)}, u32[]{:S(2)}) collective-permute-start(f32[896]{0:T(1024)S(1)} %pad_maximum_fusion.8), channel_id=1, source_target_pairs={{0,2},{1,3},{2,0},{3,1},{4,6},{5,7},{6,4},{7,5},{8,10},{9,11},{10,... | collective-permute-start | bytes 10760 | tf_op jit(solution)/shard_map/ppermute | solution.py:20
  15.5 16.9 %collective-permute-start.8 = (f32[896]{0:T(1024)S(1)}, f32[896]{0:T(1024)S(1)}, u32[]{:S(2)}, u32[]{:S(2)}) collective-permute-start(f32[896]{0:T(1024)S(1)} %pad_maximum_fusion.8), channel_id=1, source_target_pairs={{0,3},{1,0},{2,1},{3,2},{4,7},{5,4},{6,5},{7,6},{8,11},{9,8},{10,9... | collective-permute-start | bytes 10760 | tf_op jit(solution)/shard_map/ppermute | solution.py:20
  18.2 14.2 %collective-permute-start.9 = (f32[896]{0:T(1024)S(1)}, f32[896]{0:T(1024)S(1)}, u32[]{:S(2)}, u32[]{:S(2)}) collective-permute-start(f32[896]{0:T(1024)S(1)} %pad_maximum_fusion.8), channel_id=1, source_target_pairs={{0,1},{1,2},{2,3},{3,0},{4,5},{5,6},{6,7},{7,4},{8,9},{9,10},{10,1... | collective-permute-start | bytes 10760 | tf_op jit(solution)/shard_map/ppermute | solution.py:20
  22.6 6.1 %collective-permute-start.2 = (bf16[128,256]{1,0:T(8,128)(2,1)S(1)}, bf16[128,256]{1,0:T(8,128)(2,1)S(1)}, u32[]{:S(2)}, u32[]{:S(2)}) collective-permute-start(bf16[128,256]{1,0:T(8,128)(2,1)S(1)} %pad_maximum_fusion.2), channel_id=1, source_target_pairs={{0,1},{1,2},{2,3},{3,0},{4,5},{5,6},{6,7},{7,4},{8,9},{9,10},{10,1... | collective-permute-start | bytes 196616 | tf_op jit(solution)/shard_map/ppermute | solution.py:20
  28.8 7.3 %collective-permute-start.3 = (bf16[3,64,256]{2,1,0:T(8,128)(2,1)S(1)}, bf16[3,64,256]{2,1,0:T(8,128)(2,1)S(1)}, u32[]{:S(2)}, u32[]{:S(2)}) collective-permute-start(bf16[3,64,256]{2,1,0:T(8,128)(2,1)S(1)} %get-tuple-element.28), channel_id=1, source_target_pairs={{4,8},{12,16},{20,24},{8,4},{16,12},{24,20},{5,9},{13,17},{21,25},... | collective-permute-start | bytes 294920 | tf_op jit(solution)/shard_map/ppermute | solution.py:164
  29.5 6.6 %collective-permute-start.4 = (bf16[3,64,256]{2,1,0:T(8,128)(2,1)S(1)}, bf16[3,64,256]{2,1,0:T(8,128)(2,1)S(1)}, u32[]{:S(2)}, u32[]{:S(2)}) collective-permute-start(bf16[3,64,256]{2,1,0:T(8,128)(2,1)S(1)} %get-tuple-element.27), channel_id=1, source_target_pairs={{0,4},{8,12},{16,20},{24,28},{4,0},{12,8},{20,16},{28,24},{1,5},{9... | collective-permute-start | bytes 294920 | tf_op jit(solution)/shard_map/ppermute | solution.py:164
  32.4 2.3 %copy-start.1 = (bf16[9,256,1024]{2,1,0:T(8,128)(2,1)S(1)}, bf16[9,256,1024]{2,1,0:T(8,128)(2,1)}, u32[]{:S(2)}) copy-start(bf16[9,256,1024]{2,1,0:T(8,128)(2,1)} %copy-done) | copy-start | bytes 14155780
  36.0 8.7 %collective-permute-start.5 = (bf16[384,256]{1,0:T(8,128)(2,1)S(1)}, bf16[384,256]{1,0:T(8,128)(2,1)S(1)}, u32[]{:S(2)}, u32[]{:S(2)}) collective-permute-start(bf16[384,256]{1,0:T(8,128)(2,1)S(1)} %slice.159), channel_id=1, source_target_pairs={{0,1},{1,2},{2,3},{3,0},{4,5},{5,6},{6,7},{7,4},{8,9},{9,10},{10,1... | collective-permute-start | bytes 589832 | tf_op jit(solution)/shard_map/ppermute | solution.py:20
  38.4 44.7 %copy-start.4 = (f32[256]{0:T(256)S(1)}, f32[256]{0:T(256)}, u32[]{:S(2)}) copy-start(f32[256]{0:T(256)} %param.13) | copy-start | bytes 3076
  46.0 5.4 %collective-permute-start.11 = (f32[1,512]{1,0:T(1,128)S(1)}, f32[1,512]{1,0:T(1,128)S(1)}, u32[]{:S(2)}, u32[]{:S(2)}) collective-permute-start(f32[1,512]{1,0:T(1,128)S(1)} %get-tuple-element.8), channel_id=1, source_target_pairs={{0,1},{1,2},{2,3},{3,0},{4,5},{5,6},{6,7},{7,4},{8,9},{9,10},{10,1... | collective-permute-start | bytes 6152 | tf_op jit(solution)/shard_map/ppermute | solution.py:20
  46.0 5.4 %collective-permute-start.12 = (f32[1,512]{1,0:T(1,128)S(1)}, f32[1,512]{1,0:T(1,128)S(1)}, u32[]{:S(2)}, u32[]{:S(2)}) collective-permute-start(f32[1,512]{1,0:T(1,128)S(1)} %get-tuple-element.8), channel_id=1, source_target_pairs={{0,2},{1,3},{2,0},{3,1},{4,6},{5,7},{6,4},{7,5},{8,10},{9,11},{10,... | collective-permute-start | bytes 6152 | tf_op jit(solution)/shard_map/ppermute | solution.py:20
  46.1 5.8 %collective-permute-start.13 = (f32[1,512]{1,0:T(1,128)S(1)}, f32[1,512]{1,0:T(1,128)S(1)}, u32[]{:S(2)}, u32[]{:S(2)}) collective-permute-start(f32[1,512]{1,0:T(1,128)S(1)} %get-tuple-element.8), channel_id=1, source_target_pairs={{0,3},{1,0},{2,1},{3,2},{4,7},{5,4},{6,5},{7,6},{8,11},{9,8},{10,9... | collective-permute-start | bytes 6152 | tf_op jit(solution)/shard_map/ppermute | solution.py:20
  52.3 8.2 %collective-permute-start.14 = (bf16[512,256]{1,0:T(8,128)(2,1)S(1)}, bf16[512,256]{1,0:T(8,128)(2,1)S(1)}, u32[]{:S(2)}, u32[]{:S(2)}) collective-permute-start(bf16[512,256]{1,0:T(8,128)(2,1)S(1)} %shard_map.78.refs_2_), channel_id=1, source_target_pairs={{0,1},{1,2},{2,3},{3,0},{4,5},{5,6},{6,7},{7,4},{8,9},{9,10},{10,1... | collective-permute-start | bytes 786440 | tf_op jit(solution)/shard_map/ppermute | solution.py:20
  60.5 6.2 %collective-permute-start.20 = (bf16[2,64,256]{2,1,0:T(8,128)(2,1)S(1)}, bf16[2,64,256]{2,1,0:T(8,128)(2,1)S(1)}, u32[]{:S(2)}, u32[]{:S(2)}) collective-permute-start(bf16[2,64,256]{2,1,0:T(8,128)(2,1)S(1)} %get-tuple-element.32), channel_id=1, source_target_pairs={{4,8},{12,16},{20,24},{8,4},{16,12},{24,20},{5,9},{13,17},{21,25},... | collective-permute-start | bytes 196616 | tf_op jit(solution)/shard_map/ppermute | solution.py:164
  61.2 5.5 %collective-permute-start.21 = (bf16[2,64,256]{2,1,0:T(8,128)(2,1)S(1)}, bf16[2,64,256]{2,1,0:T(8,128)(2,1)S(1)}, u32[]{:S(2)}, u32[]{:S(2)}) collective-permute-start(bf16[2,64,256]{2,1,0:T(8,128)(2,1)S(1)} %get-tuple-element.31), channel_id=1, source_target_pairs={{0,4},{8,12},{16,20},{24,28},{4,0},{12,8},{20,16},{28,24},{1,5},{9... | collective-permute-start | bytes 196616 | tf_op jit(solution)/shard_map/ppermute | solution.py:164
  64.1 10.1 %collective-permute-start.15 = (bf16[512,256]{1,0:T(8,128)(2,1)S(1)}, bf16[512,256]{1,0:T(8,128)(2,1)S(1)}, u32[]{:S(2)}, u32[]{:S(2)}) collective-permute-start(bf16[512,256]{1,0:T(8,128)(2,1)S(1)} %collective-permute-done.14.refs_2_), channel_id=1, source_target_pairs={{0,1},{1,2},{2,3},{3,0},{4,5},{5,6},{6,7},{7,4},{8,9},{9,10},{10,1... | collective-permute-start | bytes 786440 | tf_op jit(solution)/shard_map/ppermute | solution.py:20
  74.2 6.1 %collective-permute-start.16 = (bf16[128,256]{1,0:T(8,128)(2,1)S(1)}, bf16[128,256]{1,0:T(8,128)(2,1)S(1)}, u32[]{:S(2)}, u32[]{:S(2)}) collective-permute-start(bf16[128,256]{1,0:T(8,128)(2,1)S(1)} %pad_maximum_fusion.3), channel_id=1, source_target_pairs={{0,1},{1,2},{2,3},{3,0},{4,5},{5,6},{6,7},{7,4},{8,9},{9,10},{10,1... | collective-permute-start | bytes 196616 | tf_op jit(solution)/shard_map/ppermute | solution.py:20
  80.4 4.6 %collective-permute-start.17 = (bf16[2,64,256]{2,1,0:T(8,128)(2,1)S(1)}, bf16[2,64,256]{2,1,0:T(8,128)(2,1)S(1)}, u32[]{:S(2)}, u32[]{:S(2)}) collective-permute-start(bf16[2,64,256]{2,1,0:T(8,128)(2,1)S(1)} %get-tuple-element.36), channel_id=1, source_target_pairs={{4,8},{12,16},{20,24},{8,4},{16,12},{24,20},{5,9},{13,17},{21,25},... | collective-permute-start | bytes 196616 | tf_op jit(solution)/shard_map/ppermute | solution.py:164
  81.1 3.9 %collective-permute-start.18 = (bf16[2,64,256]{2,1,0:T(8,128)(2,1)S(1)}, bf16[2,64,256]{2,1,0:T(8,128)(2,1)S(1)}, u32[]{:S(2)}, u32[]{:S(2)}) collective-permute-start(bf16[2,64,256]{2,1,0:T(8,128)(2,1)S(1)} %get-tuple-element.35), channel_id=1, source_target_pairs={{0,4},{8,12},{16,20},{24,28},{4,0},{12,8},{20,16},{28,24},{1,5},{9... | collective-permute-start | bytes 196616 | tf_op jit(solution)/shard_map/ppermute | solution.py:164
  84.9 8.7 %collective-permute-start.19 = (bf16[384,256]{1,0:T(8,128)(2,1)S(1)}, bf16[384,256]{1,0:T(8,128)(2,1)S(1)}, u32[]{:S(2)}, u32[]{:S(2)}) collective-permute-start(bf16[384,256]{1,0:T(8,128)(2,1)S(1)} %slice.172), channel_id=1, source_target_pairs={{0,1},{1,2},{2,3},{3,0},{4,5},{5,6},{6,7},{7,4},{8,9},{9,10},{10,1... | collective-permute-start | bytes 589832 | tf_op jit(solution)/shard_map/ppermute | solution.py:20

commit v3 on v0

v3 whole, which is shorter than its diff:
```python
import jax
import jax.numpy as jnp
from jax import lax
from jax.experimental import pallas as pl
from jax.experimental.pallas import tpu as pltpu
from jax.sharding import PartitionSpec as P

WIDTH = 64
LANES = 128


def shift_along(block, axis, step):
    count = lax.axis_size(axis)
    pairs = [(i, i + step) for i in range(count) if 0 <= i + step < count]
    return lax.ppermute(block, axis, pairs)


VMEM = pl.BlockSpec(memory_space=pltpu.VMEM)
HBM = pl.BlockSpec(memory_space=pltpu.HBM)
PARAMS = pltpu.CompilerParams(vmem_limit_bytes=20 << 20)


def column_of(row):
    return jnp.broadcast_to(row, (LANES, row.shape[1])).T[:, :1]


def row_of(column):
    return jnp.broadcast_to(column, (column.shape[0], LANES)).T[:1]


def silu(values):
    return values / (1.0 + jnp.exp(-values))


def filter_copies(frame, weights, taps, sems):
    return [
        pltpu.make_async_copy(weights.at[frame, q, s], taps.at[q * 3 + s], sems.at[q * 3 + s])
        for q in range(3)
        for s in range(3)
    ]


def fetch_kernel(frame, weights, taps, sems):
    copies = filter_copies(frame, weights, taps, sems)
    for copy in copies:
        copy.start()
    for copy in copies:
        copy.wait()


def fetch(weights):
    outs, total = weights.shape[3:]
    return pl.pallas_call(
        lambda *refs: fetch_kernel(weights.shape[0] - 1, *refs),
        out_shape=pltpu.VMEM((9, outs, total), weights.dtype),
        in_specs=[HBM],
        out_specs=VMEM,
        scratch_shapes=[pltpu.SemaphoreType.DMA((9,))],
        compiler_params=PARAMS,
    )(pltpu.with_memory_space_constraint(weights, pltpu.HBM))


def shifted(values):
    cells = values.shape[0]
    column = lax.broadcasted_iota(jnp.int32, (cells, 1), 0) % WIDTH
    before = jnp.where(column == 0, 0.0, pltpu.roll(values, 1, 0))
    after = jnp.where(column == WIDTH - 1, 0.0, pltpu.roll(values, cells - 1, 0))
    return [part.astype(jnp.bfloat16) for part in (before, values, after)]


def matmul(left, right):
    return lax.dot_general(
        jnp.concatenate(left, axis=1),
        jnp.concatenate(right, axis=1),
        (((1,), (1,)), ((), ())),
        preferred_element_type=jnp.float32,
    )


def steps_of(count):
    return sorted(range(1, count), key=lambda step: (step == count // 2, step != count - 1, step))


def owner_of(k):
    return lax.axis_index("chan") ^ [0, *steps_of(lax.axis_size("chan"))][k]


def lanes_of(owner, width):
    return pl.ds(pl.multiple_of(owner * width, width), width)


def main_taps(block, taps, owner, acts):
    cells, width = block.shape
    zeros = jnp.zeros((WIDTH, width), acts.dtype)
    for s, part in enumerate(shifted(block.astype(jnp.float32))):
        acts[s, :WIDTH] = zeros
        acts[s, WIDTH : WIDTH + cells] = part
        acts[s, WIDTH + cells :] = zeros
    lanes = lanes_of(owner, width)
    left = [acts[s, q * WIDTH : q * WIDTH + cells] for q in range(3) for s in range(3)]
    return matmul(left, [taps[t, :, lanes] for t in range(9)])


def edge_taps(block, taps, owner):
    cells, width = block.shape
    lanes = lanes_of(owner, width)
    above = matmul(shifted(block[:WIDTH].astype(jnp.float32)), [taps[6 + s, :, lanes] for s in range(3)])
    low = shifted(block[cells - WIDTH :].astype(jnp.float32))
    return above, matmul(low, [taps[s, :, lanes] for s in range(3)])


def send_kernel(source, note, out, gain, sems):
    width, cells = source.shape
    copies = [
        pltpu.make_async_copy(source, out.at[:width], sems.at[0]),
        pltpu.make_async_copy(note, gain, sems.at[1]),
    ]
    for copy in copies:
        copy.start()
    copies[1].wait()
    parts, rest = [], gain[...]
    for _ in range(3):
        parts.append(rest.astype(jnp.bfloat16).astype(jnp.float32))
        rest = rest - parts[-1]
    rows = jnp.concatenate([*parts, jnp.zeros((5, width), jnp.float32)], axis=0)
    if cells > width:
        rows = jnp.concatenate([rows, jnp.zeros((8, cells - width), jnp.float32)], axis=1)
    out[width:] = rows.astype(out.dtype)
    copies[0].wait()


def to_send(block, gain):
    width, cells = block.shape
    return pl.pallas_call(
        send_kernel,
        out_shape=pltpu.VMEM((width + 8, cells), block.dtype),
        in_specs=[HBM] * 2,
        out_specs=VMEM,
        scratch_shapes=[pltpu.VMEM(gain.shape, gain.dtype), pltpu.SemaphoreType.DMA((2,))],
        compiler_params=PARAMS,
    )(*[pltpu.with_memory_space_constraint(value, pltpu.HBM) for value in (block, gain)])


def first_kernel(total, count, *refs):
    blocks, (taps, out, first, second) = refs[:count], refs[count:]
    width = blocks[0].shape[0] - 8

    def block(k):
        return blocks[k][:width].astype(jnp.float32)

    squares = sum(jnp.sum(block(k) * block(k), axis=0, keepdims=True) for k in range(count))
    inverse = column_of(1.0 / jnp.sqrt(squares / total + 1e-6))
    for k in range(count):
        note = blocks[k][width:, :width].astype(jnp.float32)
        gain = (note[0:1] + note[1:2]) + note[2:3]
        out[k] = silu(block(k).T * gain * inverse).astype(out.dtype)
    parts = [edge_taps(out[k], taps, owner_of(k)) for k in range(count)]
    first[...], second[...] = to_swap(sum(p[0] for p in parts), sum(p[1] for p in parts))


def first_act(blocks, taps):
    outs, total = taps.shape[1:]
    width, cells = blocks[0].shape[0] - 8, blocks[0].shape[1]
    count = len(blocks)
    edge = jax.ShapeDtypeStruct((WIDTH, outs), jnp.float32)
    return pl.pallas_call(
        lambda *refs: first_kernel(total, count, *refs),
        out_shape=[
            jax.ShapeDtypeStruct((count, cells, width), jnp.bfloat16),
            edge,
            edge,
        ],
        in_specs=[VMEM] * (count + 1),
        out_specs=[VMEM] * 3,
        compiler_params=PARAMS,
    )(*blocks, taps)


def first_main_kernel(blocks, taps, out, acts):
    for k in range(blocks.shape[0]):
        part = main_taps(blocks[k], taps, owner_of(k), acts.at[k % 2])
        out[...] = part if k == 0 else out[...] + part


def first_main(blocks, taps):
    _, cells, width = blocks.shape
    return pl.pallas_call(
        first_main_kernel,
        out_shape=jax.ShapeDtypeStruct((cells, taps.shape[1]), jnp.float32),
        in_specs=[VMEM] * 2,
        out_specs=VMEM,
        scratch_shapes=[pltpu.VMEM((2, 3, cells + 2 * WIDTH, width), jnp.bfloat16)],
        compiler_params=PARAMS,
    )(blocks, taps)


def edge_kernel(k, block, taps, *refs):
    before, outs = refs[:-2], refs[-2:]
    parts = edge_taps(block[...], taps, owner_of(k))
    if before:
        parts = [ref[...] + part for ref, part in zip(before, parts)]
    outs[0][...], outs[1][...] = to_swap(*parts)


def main_kernel(k, block, taps, *refs):
    before, out, acts = refs[:-2], refs[-2], refs[-1]
    part = main_taps(block[...], taps, owner_of(k), acts)
    out[...] = before[0][...] + part if before else part


def both_kernel(k, block, taps, *refs):
    before, outs, acts = refs[:-4], refs[-4:-1], refs[-1]
    parts = [main_taps(block[...], taps, owner_of(k), acts), *edge_taps(block[...], taps, owner_of(k))]
    for place, part in enumerate(parts):
        outs[place][...] = before[place][...] + part if before else part


def second_part(kernel, k, block, taps, before):
    cells, width = block.shape
    sizes = {main_kernel: [cells], edge_kernel: [WIDTH] * 2, both_kernel: [cells, WIDTH, WIDTH]}[kernel]
    operands = [block, taps, *before]
    acts = pltpu.VMEM((3, cells + 2 * WIDTH, width), jnp.bfloat16)
    return pl.pallas_call(
        lambda *refs: kernel(k, *refs),
        out_shape=[jax.ShapeDtypeStruct((size, taps.shape[1]), jnp.float32) for size in sizes],
        in_specs=[VMEM] * len(operands),
        out_specs=[VMEM] * len(sizes),
        input_output_aliases={2 + i: i for i in range(len(before))},
        scratch_shapes=[] if kernel is edge_kernel else [acts],
        compiler_params=PARAMS,
    )(*operands)


def to_swap(above, below):
    even = lax.axis_index("rows") % 2 == 0
    return jnp.where(even, below, above), jnp.where(even, above, below)


def joined(main, first, second, bias):
    row = lax.axis_index("rows")
    even, top, low = row % 2 == 0, row == 0, row == lax.axis_size("rows") - 1
    above = jnp.where(even, second[...], first[...])
    below = jnp.where(even, first[...], second[...])
    above, below = jnp.where(top, 0.0, above), jnp.where(low, 0.0, below)
    end = main.shape[0] - WIDTH
    rows = [main[:WIDTH] + above, main[WIDTH:end], main[end:] + below]
    return jnp.concatenate(rows, axis=0) + bias[...]


def middle_kernel(main, first, second, bias, out, squares):
    middle = joined(main, first, second, bias)
    out[...] = middle
    squares[...] = row_of(jnp.sum(middle * middle, axis=1, keepdims=True))


def out_kernel(main, first, second, bias, source, out):
    result = joined(main, first, second, bias).T + source[...].astype(jnp.float32)
    out[...] = result.astype(out.dtype)


def act_kernel(total, values, gain, *refs):
    sums, out = refs[:-1], refs[-1]
    inverse = column_of(1.0 / jnp.sqrt(sum(ref[...] for ref in sums) / total + 1e-6))
    out[...] = silu(values[...] * gain[...] * inverse).astype(out.dtype)


def act(values, gain, sums, total):
    return pl.pallas_call(
        lambda *refs: act_kernel(total, *refs),
        out_shape=jax.ShapeDtypeStruct(values.shape, jnp.bfloat16),
        in_specs=[VMEM] * (2 + len(sums)),
        out_specs=VMEM,
        compiler_params=PARAMS,
    )(values, gain, *sums)


def with_row_neighbours(sends):
    count = lax.axis_size("rows")
    rounds = []
    for begin, send in enumerate(sends):
        pairs = [(i, (i + 1) % count) for i in range(begin, count, 2)]
        rounds.append(lax.ppermute(send, "rows", pairs + [(b, a) for a, b in pairs]))
    return rounds


def swap(value, step):
    return lax.ppermute(value, "chan", [(i, i ^ step) for i in range(lax.axis_size("chan"))])


def gathered(block):
    blocks = {0: block}
    for step in steps_of(lax.axis_size("chan")):
        blocks[step] = swap(block, step)
    return blocks


def resident(
    features, gain_first, weight_first, bias_first, gain_second, weight_second, bias_second
):
    channels, frames, cells = features.shape
    total = weight_first.shape[4]
    count = lax.axis_size("chan")
    source = features.reshape(channels, cells)
    taps = fetch(weight_first)
    blocks = gathered(to_send(source, gain_first.reshape(1, -1)))
    blocks, *edges = first_act(list(blocks.values()), taps)
    edges = with_row_neighbours(edges)
    main = first_main(blocks, taps)
    middle, squares = pl.pallas_call(
        middle_kernel,
        out_shape=[
            jax.ShapeDtypeStruct((cells, channels), jnp.float32),
            jax.ShapeDtypeStruct((1, cells), jnp.float32),
        ],
        in_specs=[VMEM] * 4,
        out_specs=[VMEM] * 2,
        compiler_params=PARAMS,
    )(main, *edges, bias_first.reshape(1, -1))
    others = [swap(squares, step) for step in range(count - 1, 0, -1)]
    block = act(middle, gain_second.reshape(1, -1), [squares, *others], total)
    taps = fetch(weight_second)
    blocks = gathered(block)
    parts = ()
    for k, step in enumerate(blocks):
        part = lambda kernel, before: second_part(kernel, k, blocks[step], taps, before)
        if k < count - 1:
            parts = part(both_kernel, parts)
    edges = part(edge_kernel, parts[1:])
    edges = with_row_neighbours(edges)
    main = part(main_kernel, parts[:1])
    out = pl.pallas_call(
        out_kernel,
        out_shape=jax.ShapeDtypeStruct((channels, cells), features.dtype),
        in_specs=[VMEM] * 5,
        out_specs=VMEM,
        compiler_params=PARAMS,
    )(main[0], *edges, bias_second.reshape(1, -1), source)
    return out.reshape(channels, frames, cells)


def padded(block, width):
    low = shift_along(block[..., block.shape[-1] - width :], "rows", 1)
    high = shift_along(block[..., :width], "rows", -1)
    return jnp.concatenate([low, block, high], axis=-1)


def activate(values, gain, total):
    mean_sq = lax.psum(jnp.sum(values * values, axis=0, keepdims=True), "chan") / total
    return jax.nn.silu(values * gain[:, None, None] / jnp.sqrt(mean_sq + 1e-06)).astype(jnp.bfloat16)


def convolve(block, kernel):
    whole = padded(lax.all_gather(block, "chan", axis=0, tiled=True), WIDTH)
    channels, frames, cells = whole.shape
    grid = whole.reshape(1, channels, frames, cells // WIDTH, WIDTH)
    result = lax.conv_general_dilated(
        grid,
        kernel,
        (1, 1, 1),
        ((2, 0), (0, 0), (1, 1)),
        dimension_numbers=("NCDHW", "DHWOI", "NCDHW"),
        preferred_element_type=jnp.float32,
    )
    return result[0].reshape(kernel.shape[3], frames, cells - 2 * WIDTH)


def general(features, gain_first, weight_first, bias_first, gain_second, weight_second, bias_second):
    total = weight_first.shape[4]
    source = features.astype(jnp.float32)
    middle = convolve(activate(source, gain_first, total), weight_first) + bias_first[:, None, None]
    result = convolve(activate(middle, gain_second, total), weight_second)
    return (source + result + bias_second[:, None, None]).astype(jnp.bfloat16)


def on_device(
    features, gain_first, weight_first, bias_first, gain_second, weight_second, bias_second
):
    channels, frames, cells = features.shape
    chan, rows = lax.axis_size("chan"), lax.axis_size("rows")
    narrow = channels % LANES or cells < 3 * WIDTH or channels > cells
    if frames != 1 or narrow or chan < 2 or chan & (chan - 1) or rows % 2:
        return general(
            features, gain_first, weight_first, bias_first, gain_second, weight_second, bias_second
        )
    out = resident(
        features, gain_first, weight_first, bias_first, gain_second, weight_second, bias_second
    )
    return out


def solution(mesh):
    in_specs = (
        P("chan", None, "rows"),
        P("chan"),
        P(None, None, None, "chan", None),
        P("chan"),
        P("chan"),
        P(None, None, None, "chan", None),
        P("chan"),
    )
    return jax.shard_map(
        on_device, mesh=mesh, in_specs=in_specs, out_specs=P("chan", None, "rows"), check_vma=False
    )
```

time: 155 us -> 73.9 us (0.48)
  waiting for transfers between devices: 67 us -> 40.8 us
  matrix products: 23.7 us -> 0 us
  blocking collectives: 17.4 us -> 0 us
  Pallas kernels: 0 us -> 15.9 us
  local copies, waits for them, and re-layouts: 15.4 us -> 0.03 us
  between operations: 13.7 us -> 0.15 us
  other arithmetic: 5.62 us -> 0 us
  starting transfers between devices: 11.3 us -> 16 us
    all_gather x2 -> x0, waiting for transfers between devices: 56.6 us -> none  [convolve(): whole = lax.all_gather(block, 'chan', axis=0, tiled=True)]
    ppermute x4 -> x13, waiting for transfers between devices: 10.3 us -> 40.8 us  [the longest x9 36.9 us: swap(): lax.ppermute(value, 'chan', [(i, i ^ step) for i in range(lax.axis_size('...]
    conv_general_dilated x2 -> x0, matrix products: 23.7 us -> none  [conv_rows(): lax.conv_general_dilated(grid, kernel, (1, 1, 1), ((2, 0), (0, 0), (1, 1)...]
    psum x2 -> x0, blocking collectives: 17.4 us -> none  [activate(): totals = lax.psum(jnp.sum(values * values, axis=0), 'chan')]
    pallas_call x0 -> x13, Pallas kernels: none -> 15.9 us  [the longest x2 4.76 us: fetch(): pl.pallas_call(lambda *refs: fetch_kernel(weights.shape[0] - 1, *refs), o...]
    conv_general_dilated x12 -> x0, local copies, waits for them, and re-layouts: 7.92 us -> none  [conv_rows(): lax.conv_general_dilated(grid, kernel, (1, 1, 1), ((2, 0), (0, 0), (1, 1)...]
    ppermute x4 -> x13, starting transfers between devices: 11.3 us -> 16 us  [the longest x9 11 us: swap(): lax.ppermute(value, 'chan', [(i, i ^ step) for i in range(lax.axis_size('...]
    reshape x2 -> x0, local copies, waits for them, and re-layouts: 3.02 us -> none  [conv_rows(): grid = data.reshape(1, channels, frames, rows_in, WIDTH)]
  transfers between devices with their start and end apart: 6 -> 13, of which waited for: 4 -> 10; matrix products, arithmetic and copies ran while one was open for 0% -> 0% of each run, Pallas kernels for 0% -> 16%
where the time goes in v3:
time: 73.9 us; the launch traced here: 72.7 us
  waiting for transfers between devices  40.8 us (55%)
  starting transfers between devices  16 us (22%)
  Pallas kernels  15.9 us (22%)
    ppermute x9, waiting for transfers between devices, swap(): lax.ppermute(value, 'chan', [(i, i ^ step) for i in range(lax.axis_size('...  36.9 us
    ppermute x9, starting transfers between devices, swap(): lax.ppermute(value, 'chan', [(i, i ^ step) for i in range(lax.axis_size('...  11 us
    ppermute x4, starting transfers between devices, with_row_neighbours(): lax.ppermute(send, 'rows', pairs + [(b, a) for a, b in pairs])  5 us
    pallas_call x2, Pallas kernels, fetch(): pl.pallas_call(lambda *refs: fetch_kernel(weights.shape[0] - 1, *refs), o...  4.76 us
    pallas_call x5, Pallas kernels, second_part(): pl.pallas_call(lambda *refs: kernel(k, *refs), out_shape=[jax.ShapeDtypeS...  4.35 us
    ppermute x4, waiting for transfers between devices, with_row_neighbours(): lax.ppermute(send, 'rows', pairs + [(b, a) for a, b in pairs])  3.88 us
    pallas_call x1, Pallas kernels, first_main(): pl.pallas_call(first_main_kernel, out_shape=jax.ShapeDtypeStruct((cells,...  2.66 us
    pallas_call x1, Pallas kernels, first_act(): pl.pallas_call(lambda *refs: first_kernel(total, count, *refs), out_shape...  1.67 us
  transfers between devices with their start and end apart: 13, of which 10 were waited for; matrix products, arithmetic and copies ran while one was open for 0% of the time, Pallas kernels for 16%

profile of v3, /device:TPU:3, one launch (start us, length us, event | category | flops | bytes accessed | tf_op | source)
XLA Modules:
  0.0 72.7 jit_solution(6531773070052443281)
XLA Ops:
  0.0 1.0 %shard_map.73.refs_0_ = bf16[264,512]{1,0:T(8,128)(2,1)S(1)} custom-call(bf16[256,512]{1,0:T(8,128)(2,1)} %bitcast.6, f32[1,256]{1,0:T(1,128)} %bitcast.11), custom_call_target="tpu_custom_call" | custom-call | tf_op jit(solution)/shard_map/pallas_call | solution.py:134
  1.0 0.0 copy-start.1
  1.0 0.0 copy-start.2
  1.0 3.4 %collective-permute-start = (bf16[264,512]{1,0:T(8,128)(2,1)S(1)}, bf16[264,512]{1,0:T(8,128)(2,1)S(1)}, u32[]{:S(2)}, u32[]{:S(2)}) collective-permute-start(bf16[264,512]{1,0:T(8,128)(2,1)S(1)} %shard_map.73.refs_0_), channel_id=1, source_target_pairs={{0,3},{1,2},{2,1},{3,0},{4,7},{5,6},{6,5},{7,4},{8,11},{9,10},{10,... | collective-permute-start | bytes 811016 | tf_op jit(solution)/shard_map/ppermute | solution.py:287
  4.4 0.0 collective-permute-start.1
  4.4 0.4 collective-permute-start.2
  4.7 2.4 %shard_map.74.refs_4_.taps = bf16[9,256,1024]{2,1,0:T(8,128)(2,1)S(1)} custom-call(bf16[3,3,3,256,1024]{4,3,2,1,0:T(8,128)(2,1)} %refs_0_.2), custom_call_target="tpu_custom_call" | custom-call | tf_op jit(solution)/shard_map/pallas_call | solution.py:53
  7.1 3.3 %collective-permute-done.refs_1_ = bf16[264,512]{1,0:T(8,128)(2,1)S(1)} collective-permute-done((bf16[264,512]{1,0:T(8,128)(2,1)S(1)}, bf16[264,512]{1,0:T(8,128)(2,1)S(1)}, u32[]{:S(2)}, u32[]{:S(2)}) %collective-permute-start) | collective-permute-done | bytes 270368 | tf_op jit(solution)/shard_map/ppermute | solution.py:287
  10.5 7.6 %collective-permute-done.1.refs_2_ = bf16[264,512]{1,0:T(8,128)(2,1)S(1)} collective-permute-done((bf16[264,512]{1,0:T(8,128)(2,1)S(1)}, bf16[264,512]{1,0:T(8,128)(2,1)S(1)}, u32[]{:S(2)}, u32[]{:S(2)}) %collective-permute-start.1) | collective-permute-done | bytes 270368 | tf_op jit(solution)/shard_map/ppermute | solution.py:287
  18.1 8.9 %collective-permute-done.2.refs_3_ = bf16[264,512]{1,0:T(8,128)(2,1)S(1)} collective-permute-done((bf16[264,512]{1,0:T(8,128)(2,1)S(1)}, bf16[264,512]{1,0:T(8,128)(2,1)S(1)}, u32[]{:S(2)}, u32[]{:S(2)}) %collective-permute-start.2) | collective-permute-done | bytes 270368 | tf_op jit(solution)/shard_map/ppermute | solution.py:287
  27.0 1.7 %shard_map.75 = (bf16[4,512,256]{2,1,0:T(8,128)(2,1)S(1)}, f32[64,256]{1,0:T(8,128)S(1)}, f32[64,256]{1,0:T(8,128)S(1)}) custom-call(bf16[264,512]{1,0:T(8,128)(2,1)S(1)} %shard_map.73.refs_0_, bf16[264,512]{1,0:T(8,128)(2,1)S(1)} %collective-permute-done.refs_1_, bf16[264,512]{1,0:T(8,128)(2,1)S(1)} %collective-permute-done.1.refs_2_, ...), custom_call_target="tpu_custom_call" | custom-call | tf_op jit(solution)/shard_map/pallas_call | solution.py:166
  28.7 1.4 %collective-permute-start.3 = (f32[64,256]{1,0:T(8,128)S(1)}, f32[64,256]{1,0:T(8,128)S(1)}, u32[]{:S(2)}, u32[]{:S(2)}) collective-permute-start(f32[64,256]{1,0:T(8,128)S(1)} %get-tuple-element.22), channel_id=1, source_target_pairs={{0,4},{8,12},{16,20},{24,28},{4,0},{12,8},{20,16},{28,24},{1,5},{9... | collective-permute-start | bytes 196616 | tf_op jit(solution)/shard_map/ppermute | solution.py:282
  30.1 1.2 %collective-permute-start.4 = (f32[64,256]{1,0:T(8,128)S(1)}, f32[64,256]{1,0:T(8,128)S(1)}, u32[]{:S(2)}, u32[]{:S(2)}) collective-permute-start(f32[64,256]{1,0:T(8,128)S(1)} %get-tuple-element.23), channel_id=1, source_target_pairs={{4,8},{12,16},{20,24},{28,0},{8,4},{16,12},{24,20},{0,28},{5,9},{1... | collective-permute-start | bytes 196616 | tf_op jit(solution)/shard_map/ppermute | solution.py:282
  31.3 2.7 %shard_map.76.main = f32[512,256]{1,0:T(8,128)S(1)} custom-call(bf16[4,512,256]{2,1,0:T(8,128)(2,1)S(1)} %get-tuple-element.21.blocks, bf16[9,256,1024]{2,1,0:T(8,128)(2,1)S(1)} %shard_map.74.refs_4_.taps), custom_call_target="tpu_custom_call" | custom-call | tf_op jit(solution)/shard_map/pallas_call | solution.py:187
  33.9 0.0 collective-permute-done.3.first
  34.0 0.9 %collective-permute-done.4.second = f32[64,256]{1,0:T(8,128)S(1)} collective-permute-done((f32[64,256]{1,0:T(8,128)S(1)}, f32[64,256]{1,0:T(8,128)S(1)}, u32[]{:S(2)}, u32[]{:S(2)}) %collective-permute-start.4) | collective-permute-done | bytes 65568 | tf_op jit(solution)/shard_map/ppermute | solution.py:282
  34.8 0.0 copy-done.1
  34.8 0.2 shard_map.77
  35.0 2.2 %collective-permute-start.5 = (f32[1,512]{1,0:T(1,128)S(1)}, f32[1,512]{1,0:T(1,128)S(1)}, u32[]{:S(2)}, u32[]{:S(2)}) collective-permute-start(f32[1,512]{1,0:T(1,128)S(1)} %get-tuple-element.25.refs_2_), channel_id=1, source_target_pairs={{0,3},{1,2},{2,1},{3,0},{4,7},{5,6},{6,5},{7,4},{8,11},{9,10},{10,... | collective-permute-start | bytes 6152 | tf_op jit(solution)/shard_map/ppermute | solution.py:287
  37.3 0.0 collective-permute-start.6
  37.3 1.4 %collective-permute-start.7 = (f32[1,512]{1,0:T(1,128)S(1)}, f32[1,512]{1,0:T(1,128)S(1)}, u32[]{:S(2)}, u32[]{:S(2)}) collective-permute-start(f32[1,512]{1,0:T(1,128)S(1)} %get-tuple-element.25.refs_2_), channel_id=1, source_target_pairs={{0,1},{1,0},{2,3},{3,2},{4,5},{5,4},{6,7},{7,6},{8,9},{9,8},{10,11... | collective-permute-start | bytes 6152 | tf_op jit(solution)/shard_map/ppermute | solution.py:287
  38.6 0.7 collective-permute-done.5.refs_3_
  39.3 1.3 %collective-permute-done.6.refs_4_ = f32[1,512]{1,0:T(1,128)S(1)} collective-permute-done((f32[1,512]{1,0:T(1,128)S(1)}, f32[1,512]{1,0:T(1,128)S(1)}, u32[]{:S(2)}, u32[]{:S(2)}) %collective-permute-start.6) | collective-permute-done | bytes 2080 | tf_op jit(solution)/shard_map/ppermute | solution.py:287
  40.7 0.0 collective-permute-done.7.refs_5_
  40.7 0.0 copy-done.2
  40.7 0.3 shard_map.78.refs_0_
  41.0 1.2 %collective-permute-start.10 = (bf16[512,256]{1,0:T(8,128)(2,1)S(1)}, bf16[512,256]{1,0:T(8,128)(2,1)S(1)}, u32[]{:S(2)}, u32[]{:S(2)}) collective-permute-start(bf16[512,256]{1,0:T(8,128)(2,1)S(1)} %shard_map.78.refs_0_), channel_id=1, source_target_pairs={{0,3},{1,2},{2,1},{3,0},{4,7},{5,6},{6,5},{7,4},{8,11},{9,10},{10,... | collective-permute-start | bytes 786440 | tf_op jit(solution)/shard_map/ppermute | solution.py:287
  42.2 0.5 collective-permute-start.9
  42.7 1.9 %collective-permute-start.8 = (bf16[512,256]{1,0:T(8,128)(2,1)S(1)}, bf16[512,256]{1,0:T(8,128)(2,1)S(1)}, u32[]{:S(2)}, u32[]{:S(2)}) collective-permute-start(bf16[512,256]{1,0:T(8,128)(2,1)S(1)} %shard_map.78.refs_0_), channel_id=1, source_target_pairs={{0,2},{1,3},{2,0},{3,1},{4,6},{5,7},{6,4},{7,5},{8,10},{9,11},{10,... | collective-permute-start | bytes 786440 | tf_op jit(solution)/shard_map/ppermute | solution.py:287
  44.6 2.4 %shard_map.79.refs_1_ = bf16[9,256,1024]{2,1,0:T(8,128)(2,1)S(1)} custom-call(bf16[3,3,3,256,1024]{4,3,2,1,0:T(8,128)(2,1)} %refs_0_.3), custom_call_target="tpu_custom_call" | custom-call | tf_op jit(solution)/shard_map/pallas_call | solution.py:53
  47.0 0.0 copy-start
  47.0 0.0 copy-start.3
  47.0 1.0 %shard_map.80 = (f32[512,256]{1,0:T(8,128)S(1)}, f32[64,256]{1,0:T(8,128)S(1)}, f32[64,256]{1,0:T(8,128)S(1)}) custom-call(bf16[512,256]{1,0:T(8,128)(2,1)S(1)} %shard_map.78.refs_0_, bf16[9,256,1024]{2,1,0:T(8,128)(2,1)S(1)} %shard_map.79.refs_1_), custom_call_target="tpu_custom_call" | custom-call | tf_op jit(solution)/shard_map/pallas_call | solution.py:223
  48.1 2.3 %collective-permute-done.10.refs_0_ = bf16[512,256]{1,0:T(8,128)(2,1)S(1)} collective-permute-done((bf16[512,256]{1,0:T(8,128)(2,1)S(1)}, bf16[512,256]{1,0:T(8,128)(2,1)S(1)}, u32[]{:S(2)}, u32[]{:S(2)}) %collective-permute-start.10) | collective-permute-done | bytes 262176 | tf_op jit(solution)/shard_map/ppermute | solution.py:287
  50.4 1.0 %shard_map.81 = (f32[512,256]{1,0:T(8,128)S(1)}, f32[64,256]{1,0:T(8,128)S(1)}, f32[64,256]{1,0:T(8,128)S(1)}) custom-call(bf16[512,256]{1,0:T(8,128)(2,1)S(1)} %collective-permute-done.10.refs_0_, bf16[9,256,1024]{2,1,0:T(8,128)(2,1)S(1)} %shard_map.79.refs_1_, ...), custom_call_target="tpu_custom_call", output_to_operand_aliasing={{0}: (2, {}), {1}: (3, {}), {2}: (4, {})} | custom-call | tf_op jit(solution)/shard_map/pallas_call | solution.py:223
  51.4 5.2 %collective-permute-done.9.refs_0_ = bf16[512,256]{1,0:T(8,128)(2,1)S(1)} collective-permute-done((bf16[512,256]{1,0:T(8,128)(2,1)S(1)}, bf16[512,256]{1,0:T(8,128)(2,1)S(1)}, u32[]{:S(2)}, u32[]{:S(2)}) %collective-permute-start.9) | collective-permute-done | bytes 262176 | tf_op jit(solution)/shard_map/ppermute | solution.py:287
  56.7 1.0 %shard_map.82 = (f32[512,256]{1,0:T(8,128)S(1)}, f32[64,256]{1,0:T(8,128)S(1)}, f32[64,256]{1,0:T(8,128)S(1)}) custom-call(bf16[512,256]{1,0:T(8,128)(2,1)S(1)} %collective-permute-done.9.refs_0_, bf16[9,256,1024]{2,1,0:T(8,128)(2,1)S(1)} %shard_map.79.refs_1_, ...), custom_call_target="tpu_custom_call", output_to_operand_aliasing={{0}: (2, {}), {1}: (3, {}), {2}: (4, {})} | custom-call | tf_op jit(solution)/shard_map/pallas_call | solution.py:223
  57.7 7.4 %collective-permute-done.8.refs_0_ = bf16[512,256]{1,0:T(8,128)(2,1)S(1)} collective-permute-done((bf16[512,256]{1,0:T(8,128)(2,1)S(1)}, bf16[512,256]{1,0:T(8,128)(2,1)S(1)}, u32[]{:S(2)}, u32[]{:S(2)}) %collective-permute-start.8) | collective-permute-done | bytes 262176 | tf_op jit(solution)/shard_map/ppermute | solution.py:287
  65.2 0.4 shard_map.84
  65.6 1.7 %collective-permute-start.11 = (f32[64,256]{1,0:T(8,128)S(1)}, f32[64,256]{1,0:T(8,128)S(1)}, u32[]{:S(2)}, u32[]{:S(2)}) collective-permute-start(f32[64,256]{1,0:T(8,128)S(1)} %get-tuple-element.35), channel_id=1, source_target_pairs={{0,4},{8,12},{16,20},{24,28},{4,0},{12,8},{20,16},{28,24},{1,5},{9... | collective-permute-start | bytes 196616 | tf_op jit(solution)/shard_map/ppermute | solution.py:282
  67.2 0.8 %collective-permute-start.12 = (f32[64,256]{1,0:T(8,128)S(1)}, f32[64,256]{1,0:T(8,128)S(1)}, u32[]{:S(2)}, u32[]{:S(2)}) collective-permute-start(f32[64,256]{1,0:T(8,128)S(1)} %get-tuple-element.36), channel_id=1, source_target_pairs={{4,8},{12,16},{20,24},{28,0},{8,4},{16,12},{24,20},{0,28},{5,9},{1... | collective-permute-start | bytes 196616 | tf_op jit(solution)/shard_map/ppermute | solution.py:282
  68.0 0.8 %shard_map.83.main = f32[512,256]{1,0:T(8,128)S(1)} custom-call(bf16[512,256]{1,0:T(8,128)(2,1)S(1)} %collective-permute-done.8.refs_0_, bf16[9,256,1024]{2,1,0:T(8,128)(2,1)S(1)} %shard_map.79.refs_1_, f32[512,256]{1,0:T(8,128)S(1)} %get-tuple-element.32.refs_2_), custom_call_target="tpu_custom_call", output_to_operand_aliasing={{}: (2, {})} | custom-call | tf_op jit(solution)/shard_map/pallas_call | solution.py:223
  68.8 0.0 collective-permute-done.11.first
  68.8 3.0 %collective-permute-done.12.second = f32[64,256]{1,0:T(8,128)S(1)} collective-permute-done((f32[64,256]{1,0:T(8,128)S(1)}, f32[64,256]{1,0:T(8,128)S(1)}, u32[]{:S(2)}, u32[]{:S(2)}) %collective-permute-start.12) | collective-permute-done | bytes 65568 | tf_op jit(solution)/shard_map/ppermute | solution.py:282
  71.8 0.0 copy-done
  71.8 0.0 copy-done.3
  71.8 0.9 %shard_map.85 = bf16[256,512]{1,0:T(8,128)(2,1)} custom-call(f32[512,256]{1,0:T(8,128)S(1)} %shard_map.83.main, f32[64,256]{1,0:T(8,128)S(1)} %collective-permute-done.11.first, f32[64,256]{1,0:T(8,128)S(1)} %collective-permute-done.12.second, f32[1,256]{1,0:T(1,128)S(1)} %bitcast.10, bf16[256,512]{1,0:T(8,128)(2,1)S(1)} %bitcast.7), custom_call_target="tpu_custom_call" | custom-call | tf_op jit(solution)/shard_map/pallas_call | solution.py:331
Async XLA Ops:
  1.0 33.9 %copy-start.1 = (f32[256]{0:T(256)S(1)}, f32[256]{0:T(256)}, u32[]{:S(2)}) copy-start(f32[256]{0:T(256)} %param.10) | copy-start | bytes 3076
  1.0 39.7 %copy-start.2 = (f32[256]{0:T(256)S(1)}, f32[256]{0:T(256)}, u32[]{:S(2)}) copy-start(f32[256]{0:T(256)} %param.11) | copy-start | bytes 3076
  1.0 9.5 %collective-permute-start = (bf16[264,512]{1,0:T(8,128)(2,1)S(1)}, bf16[264,512]{1,0:T(8,128)(2,1)S(1)}, u32[]{:S(2)}, u32[]{:S(2)}) collective-permute-start(bf16[264,512]{1,0:T(8,128)(2,1)S(1)} %shard_map.73.refs_0_), channel_id=1, source_target_pairs={{0,3},{1,2},{2,1},{3,0},{4,7},{5,6},{6,5},{7,4},{8,11},{9,10},{10,... | collective-permute-start | bytes 811016 | tf_op jit(solution)/shard_map/ppermute | solution.py:287
  4.4 13.7 %collective-permute-start.1 = (bf16[264,512]{1,0:T(8,128)(2,1)S(1)}, bf16[264,512]{1,0:T(8,128)(2,1)S(1)}, u32[]{:S(2)}, u32[]{:S(2)}) collective-permute-start(bf16[264,512]{1,0:T(8,128)(2,1)S(1)} %shard_map.73.refs_0_), channel_id=1, source_target_pairs={{0,1},{1,0},{2,3},{3,2},{4,5},{5,4},{6,7},{7,6},{8,9},{9,8},{10,11... | collective-permute-start | bytes 811016 | tf_op jit(solution)/shard_map/ppermute | solution.py:287
  4.4 22.6 %collective-permute-start.2 = (bf16[264,512]{1,0:T(8,128)(2,1)S(1)}, bf16[264,512]{1,0:T(8,128)(2,1)S(1)}, u32[]{:S(2)}, u32[]{:S(2)}) collective-permute-start(bf16[264,512]{1,0:T(8,128)(2,1)S(1)} %shard_map.73.refs_0_), channel_id=1, source_target_pairs={{0,2},{1,3},{2,0},{3,1},{4,6},{5,7},{6,4},{7,5},{8,10},{9,11},{10,... | collective-permute-start | bytes 811016 | tf_op jit(solution)/shard_map/ppermute | solution.py:287
  28.7 5.3 %collective-permute-start.3 = (f32[64,256]{1,0:T(8,128)S(1)}, f32[64,256]{1,0:T(8,128)S(1)}, u32[]{:S(2)}, u32[]{:S(2)}) collective-permute-start(f32[64,256]{1,0:T(8,128)S(1)} %get-tuple-element.22), channel_id=1, source_target_pairs={{0,4},{8,12},{16,20},{24,28},{4,0},{12,8},{20,16},{28,24},{1,5},{9... | collective-permute-start | bytes 196616 | tf_op jit(solution)/shard_map/ppermute | solution.py:282
  30.1 4.7 %collective-permute-start.4 = (f32[64,256]{1,0:T(8,128)S(1)}, f32[64,256]{1,0:T(8,128)S(1)}, u32[]{:S(2)}, u32[]{:S(2)}) collective-permute-start(f32[64,256]{1,0:T(8,128)S(1)} %get-tuple-element.23), channel_id=1, source_target_pairs={{4,8},{12,16},{20,24},{28,0},{8,4},{16,12},{24,20},{0,28},{5,9},{1... | collective-permute-start | bytes 196616 | tf_op jit(solution)/shard_map/ppermute | solution.py:282
  35.0 4.3 %collective-permute-start.5 = (f32[1,512]{1,0:T(1,128)S(1)}, f32[1,512]{1,0:T(1,128)S(1)}, u32[]{:S(2)}, u32[]{:S(2)}) collective-permute-start(f32[1,512]{1,0:T(1,128)S(1)} %get-tuple-element.25.refs_2_), channel_id=1, source_target_pairs={{0,3},{1,2},{2,1},{3,0},{4,7},{5,6},{6,5},{7,4},{8,11},{9,10},{10,... | collective-permute-start | bytes 6152 | tf_op jit(solution)/shard_map/ppermute | solution.py:287
  37.3 3.4 %collective-permute-start.6 = (f32[1,512]{1,0:T(1,128)S(1)}, f32[1,512]{1,0:T(1,128)S(1)}, u32[]{:S(2)}, u32[]{:S(2)}) collective-permute-start(f32[1,512]{1,0:T(1,128)S(1)} %get-tuple-element.25.refs_2_), channel_id=1, source_target_pairs={{0,2},{1,3},{2,0},{3,1},{4,6},{5,7},{6,4},{7,5},{8,10},{9,11},{10,... | collective-permute-start | bytes 6152 | tf_op jit(solution)/shard_map/ppermute | solution.py:287
  37.3 3.4 %collective-permute-start.7 = (f32[1,512]{1,0:T(1,128)S(1)}, f32[1,512]{1,0:T(1,128)S(1)}, u32[]{:S(2)}, u32[]{:S(2)}) collective-permute-start(f32[1,512]{1,0:T(1,128)S(1)} %get-tuple-element.25.refs_2_), channel_id=1, source_target_pairs={{0,1},{1,0},{2,3},{3,2},{4,5},{5,4},{6,7},{7,6},{8,9},{9,8},{10,11... | collective-permute-start | bytes 6152 | tf_op jit(solution)/shard_map/ppermute | solution.py:287
  41.0 9.4 %collective-permute-start.10 = (bf16[512,256]{1,0:T(8,128)(2,1)S(1)}, bf16[512,256]{1,0:T(8,128)(2,1)S(1)}, u32[]{:S(2)}, u32[]{:S(2)}) collective-permute-start(bf16[512,256]{1,0:T(8,128)(2,1)S(1)} %shard_map.78.refs_0_), channel_id=1, source_target_pairs={{0,3},{1,2},{2,1},{3,0},{4,7},{5,6},{6,5},{7,4},{8,11},{9,10},{10,... | collective-permute-start | bytes 786440 | tf_op jit(solution)/shard_map/ppermute | solution.py:287
  42.2 14.4 %collective-permute-start.9 = (bf16[512,256]{1,0:T(8,128)(2,1)S(1)}, bf16[512,256]{1,0:T(8,128)(2,1)S(1)}, u32[]{:S(2)}, u32[]{:S(2)}) collective-permute-start(bf16[512,256]{1,0:T(8,128)(2,1)S(1)} %shard_map.78.refs_0_), channel_id=1, source_target_pairs={{0,1},{1,0},{2,3},{3,2},{4,5},{5,4},{6,7},{7,6},{8,9},{9,8},{10,11... | collective-permute-start | bytes 786440 | tf_op jit(solution)/shard_map/ppermute | solution.py:287
  42.7 22.4 %collective-permute-start.8 = (bf16[512,256]{1,0:T(8,128)(2,1)S(1)}, bf16[512,256]{1,0:T(8,128)(2,1)S(1)}, u32[]{:S(2)}, u32[]{:S(2)}) collective-permute-start(bf16[512,256]{1,0:T(8,128)(2,1)S(1)} %shard_map.78.refs_0_), channel_id=1, source_target_pairs={{0,2},{1,3},{2,0},{3,1},{4,6},{5,7},{6,4},{7,5},{8,10},{9,11},{10,... | collective-permute-start | bytes 786440 | tf_op jit(solution)/shard_map/ppermute | solution.py:287
  47.0 24.8 %copy-start = (bf16[256,1,512]{2,0,1:T(8,128)(2,1)S(1)}, bf16[256,1,512]{2,0,1:T(8,128)(2,1)}, u32[]{:S(2)}) copy-start(bf16[256,1,512]{2,0,1:T(8,128)(2,1)} %param.7) | copy-start | bytes 786436
  47.0 24.8 %copy-start.3 = (f32[256]{0:T(256)S(1)}, f32[256]{0:T(256)}, u32[]{:S(2)}) copy-start(f32[256]{0:T(256)} %param.13) | copy-start | bytes 3076
  65.6 3.3 %collective-permute-start.11 = (f32[64,256]{1,0:T(8,128)S(1)}, f32[64,256]{1,0:T(8,128)S(1)}, u32[]{:S(2)}, u32[]{:S(2)}) collective-permute-start(f32[64,256]{1,0:T(8,128)S(1)} %get-tuple-element.35), channel_id=1, source_target_pairs={{0,4},{8,12},{16,20},{24,28},{4,0},{12,8},{20,16},{28,24},{1,5},{9... | collective-permute-start | bytes 196616 | tf_op jit(solution)/shard_map/ppermute | solution.py:282
  67.2 4.6 %collective-permute-start.12 = (f32[64,256]{1,0:T(8,128)S(1)}, f32[64,256]{1,0:T(8,128)S(1)}, u32[]{:S(2)}, u32[]{:S(2)}) collective-permute-start(f32[64,256]{1,0:T(8,128)S(1)} %get-tuple-element.36), channel_id=1, source_target_pairs={{4,8},{12,16},{20,24},{28,0},{8,4},{16,12},{24,20},{0,28},{5,9},{1... | collective-permute-start | bytes 196616 | tf_op jit(solution)/shard_map/ppermute | solution.py:282
